TPU v7x, 32 devices: a whole 2x2x4 slice. The times are simulated.
32 devices in a mesh: groups: 2 (over x), tile: 16 (over z, y, core).
Axes of the slice: x: 2, y: 2, z: 4, core: 2. Of those that a mesh axis runs over, the one named last changes fastest.
Arguments:
- queries: bfloat16 [2048, 4096], P(('groups', 'tile')), parts along dimension 0, may hold values from -8 to 8
- key_rows: bfloat16 [2048, 4096], P(('groups', 'tile')), parts along dimension 0, may hold values from -8 to 8
- values: bfloat16 [2048, 4096], P(('groups', 'tile')), parts along dimension 0, may hold values from -6 to 6
- modulation: float32 [6, 4096], P('groups'), parts along dimension 0, may hold values from -3 to 3
- expert_in: bfloat16 [4096, 8192], P(None, 'tile'), may hold values from -0.09375 to 0.09375
- expert_out: bfloat16 [8192, 4096], P('tile'), may hold values from -0.125 to 0.125
- routes: int32 [2048, 2], P(('groups', 'tile')), parts along dimension 0, may hold values from 0 to 3, all different within a row; in each aligned block of 64 rows (0 to 63, 64 to 127, ...) at most 48 rows name the same one
- gate_fixed: int32 [2048, 2], P(('groups', 'tile')), parts along dimension 0, may hold values from 64 to 1023
Outputs:
- layer_out: bfloat16 [2048, 4096], P(('groups', 'tile')), parts along dimension 0
There are 2 independent parts, one for each index of `groups`. A program takes and returns all parts, laid end to end along the dimension named above; an argument that names none is the same for every part. Nothing has to cross between parts.
Inputs may be any that keep to these rules, and one draw needn't show every extreme that they name: `routes`: the two experts of a token differ; among the 64 tokens of one tile no expert is named more than 48 times.
All inputs are finite; a program needn't handle non-finite values.
Results may differ from a plain program's by a relative error of at most 0.011.
Values may be sent and summed in bfloat16 or wider, within the bound.
A program may use at most 128 MiB of HBM per device.

v0:
```python
import functools
import math

import jax
import jax.numpy as jnp
from jax import lax
from jax.experimental import pallas as pl
from jax.experimental.pallas import tpu as pltpu
from jax.sharding import PartitionSpec as P

HEAD_DIM = 128
D = 4096
SPLIT = 4
TILE_COLS = 8

EPSILON = 1e-06
MASKED = -1e30
MESH = pl.DeviceIdType.MESH
VMEM_LIMIT = 60 * 1024 * 1024


def when(cond, body):
    if cond is True:
        body()
    else:
        pl.when(cond)(body)


def both(a, b):
    if a is True:
        return b
    if b is True:
        return a
    return jnp.logical_and(a, b)


def remote(src, dst, send_sem, recv_sem, target):
    return pltpu.make_async_remote_copy(
        src_ref=src,
        dst_ref=dst,
        send_sem=send_sem,
        recv_sem=recv_sem,
        device_id={"tile": target},
        device_id_type=MESH,
    )


def halo_levels(n):
    grid_rows = n // TILE_COLS
    if grid_rows < 2:
        return 1
    return 2 if grid_rows == 2 else 3


def attention_kernel(
    n, rows, q_ref, k_ref, v_ref, mod_ref, att_ref, norm_ref, keys, vals, send_sem, recv_sem, own_sem,
    also=None,
):
    me = lax.axis_index("tile")
    grid_rows = n // TILE_COLS
    tile = lax.rem(me + TILE_COLS // 2, n)
    row = lax.div(tile, TILE_COLS)
    col = lax.rem(tile, TILE_COLS)
    if grid_rows < 2:
        verticals = []
    elif grid_rows == 2:
        verticals = [(1, TILE_COLS, True, 1)]
    else:
        verticals = [(1, n - TILE_COLS, row > 0, 2), (2, TILE_COLS, row < grid_rows - 1, 1)]
    sides = [(-1, col > 0), (1, col < TILE_COLS - 1)]
    here = {level: exists for level, _, exists, _ in verticals}
    here[0] = True

    def slot(level, side):
        return level * 3 + 1 + side

    def place(buf, s):
        return buf.at[pl.ds(s * rows, rows), :]

    def over(offset):
        return lax.rem(me + offset + n, n)

    half = rows // 2
    middle = TILE_COLS // 2
    crossing = {side: col == (middle if side < 0 else middle - 1) for side, _ in sides}
    two = grid_rows == 2

    def part_of(buf, s, h):
        return buf.at[pl.ds(pl.multiple_of(s * rows + h * half, half), half), :]

    own = [
        pltpu.make_async_copy(src, place(buf, slot(0, 0)), own_sem.at[i])
        for i, (src, buf) in enumerate(((k_ref, keys), (v_ref, vals)))
    ]
    for copy in own:
        copy.start()

    def beside(side):
        if not two:
            return over(side)
        return jnp.where(crossing[side], over(side + TILE_COLS), over(side))

    def level_there(level, side):
        return jnp.where(crossing[side], 1 - level, level) if two else level

    barrier = pltpu.get_barrier_semaphore()
    partners = [(over(offset), exists) for _, offset, exists, _ in verticals]
    partners += [(beside(side), exists) for side, exists in sides]
    partners += [(target, True) for target in also or []]
    for target, exists in partners:

        def greet(target=target):
            pl.semaphore_signal(barrier, inc=1, device_id={"tile": target}, device_id_type=MESH)

        when(exists, greet)
    expected = sum(1 if exists is True else jnp.where(exists, 1, 0) for _, exists in partners)
    pl.semaphore_wait(barrier, expected)

    sends = []
    pieces = [(i, h) for i in (0, 1) for h in (0, 1)]
    bufs = (keys, vals)

    def push(i, h, src, there, target, exists):
        copy = remote(
            src,
            part_of(bufs[i], there, h),
            send_sem.at[len(sends)],
            recv_sem.at[there, i * 2 + h],
            target,
        )
        when(exists, copy.start)
        sends.append((copy, exists))

    def arrived(s, exists, i, h):
        ref = part_of(bufs[i], s, h)
        when(exists, remote(ref, ref, send_sem.at[0], recv_sem.at[s, i * 2 + h], me).wait_recv)

    def own_part(i, h):
        return (k_ref, v_ref)[i].at[pl.ds(h * half, half), :]

    for i, h in pieces:
        for level, offset, exists, there in verticals:
            push(i, h, own_part(i, h), slot(there, 0), over(offset), exists)
    for i, h in pieces:
        for side, exists in sides:
            push(i, h, own_part(i, h), slot(level_there(0, side), -side), beside(side), exists)
    for s in range(3 * (1 + len(verticals))):
        level, side = s // 3, s % 3 - 1
        exists = here[level]
        for other, side_exists in sides:
            if other == side:
                exists = both(exists, side_exists)
        if exists is True:
            continue

        def clear(s=s):
            for buf in (keys, vals):
                buf[pl.ds(s * rows, rows), :] = jnp.zeros((rows, D), buf.dtype)

        pl.when(jnp.logical_not(exists))(clear)
    for i, h in pieces:
        for level, offset, exists, there in verticals:
            arrived(slot(level, 0), exists, i, h)
            for side, side_exists in sides:
                push(
                    i,
                    h,
                    part_of(bufs[i], slot(level, 0), h),
                    slot(level_there(level, side), -side),
                    beside(side),
                    both(exists, side_exists),
                )
    for copy in own:
        copy.wait()
    for i, h in pieces:
        for level, exists in sorted(here.items(), key=lambda item: item[0]):
            for side, side_exists in sides:
                arrived(slot(level, side), both(exists, side_exists), i, h)

    span = 3 * (1 + len(verticals)) * rows
    where = lax.broadcasted_iota(jnp.int32, (rows, span), 1)
    bias = jnp.zeros((rows, span), jnp.float32)
    for s in range(span // rows):
        level, side = s // 3, s % 3 - 1
        exists = here[level]
        for other, side_exists in sides:
            if other == side:
                exists = both(exists, side_exists)
        if exists is True:
            continue
        penalty = jnp.where(exists, 0.0, MASKED)
        bias = jnp.where((where >= s * rows) & (where < (s + 1) * rows), penalty, bias)
    scale = 1.0 / math.sqrt(HEAD_DIM)
    together = 8

    def heads(step, carry):
        for extra in range(together):
            at = pl.ds(pl.multiple_of((step * together + extra) * HEAD_DIM, HEAD_DIM), HEAD_DIM)
            scores = lax.dot_general(
                q_ref[:, at], keys[:, at], (((1,), (1,)), ((), ())), preferred_element_type=jnp.float32
            )
            scores = scores * scale + bias
            raised = jnp.exp(scores - jnp.max(scores, axis=-1, keepdims=True))
            probs = (raised * (1.0 / jnp.sum(raised, axis=-1, keepdims=True))).astype(jnp.bfloat16)
            att_ref[:, at] = jnp.dot(probs, vals[:, at], preferred_element_type=jnp.float32).astype(
                att_ref.dtype
            )
        return carry

    lax.fori_loop(0, D // HEAD_DIM // together, heads, 0)

    def normalise(step, carry):
        at = pl.ds(pl.multiple_of(step * 16, 16), 16)
        wide = att_ref[at, :].astype(jnp.float32)
        wide = wide - jnp.mean(wide, axis=-1, keepdims=True)
        spread = jnp.mean(wide * wide, axis=-1, keepdims=True)
        normed = wide * lax.rsqrt(spread + EPSILON)
        norm_ref[at, :] = (normed * (1.0 + mod_ref[1:2, :]) + mod_ref[0:1, :]).astype(norm_ref.dtype)
        return carry

    lax.fori_loop(0, rows // 16, normalise, 0)
    if also is not None:
        return sends
    for copy, exists in sends:
        when(exists, copy.wait_send)


def attention(queries, key_rows, values, modulation):
    n = lax.axis_size("tile")
    rows = queries.shape[0]
    levels = halo_levels(n)
    slots = 3 * levels
    vmem = pl.BlockSpec(memory_space=pltpu.VMEM)
    hbm = pl.BlockSpec(memory_space=pl.ANY)
    return pl.pallas_call(
        functools.partial(attention_kernel, n, rows),
        name="halo_attention",
        out_shape=(
            jax.ShapeDtypeStruct((rows, D), jnp.bfloat16),
            jax.ShapeDtypeStruct((rows, D), jnp.bfloat16),
        ),
        in_specs=[vmem, hbm, hbm, vmem],
        out_specs=(vmem, vmem),
        scratch_shapes=[
            pltpu.VMEM((slots * rows, D), jnp.bfloat16),
            pltpu.VMEM((slots * rows, D), jnp.bfloat16),
            pltpu.SemaphoreType.DMA((4 * (2 + 3 * (levels - 1)),)),
            pltpu.SemaphoreType.DMA((slots, 4)),
            pltpu.SemaphoreType.DMA((2,)),
        ],
        compiler_params=pltpu.CompilerParams(
            collective_id=0, has_side_effects=True, vmem_limit_bytes=VMEM_LIMIT
        ),
    )(queries, key_rows, values, modulation)


def nearest_first(p, planes):
    order = [p] + [p * 0] * (planes - 1)
    count = p * 0 + 1
    for step in range(1, planes):
        for other in (p - step, p + step):
            exists = jnp.logical_and(other >= 0, other < planes)
            for i in range(1, planes):
                order[i] = jnp.where(jnp.logical_and(exists, count == i), other, order[i])
            count = count + jnp.where(exists, 1, 0)
    return order


def positions(n):
    me = lax.axis_index("tile")
    p = lax.div(me, SPLIT)
    q = lax.rem(me, SPLIT)
    return me, p, lax.div(q, 2), lax.rem(q, 2), nearest_first(p, n // SPLIT)


def device(plane, yy, cc):
    return plane * SPLIT + yy * 2 + cc


def layer_kernel(
    n, rows, cap, q_ref, k_ref, v_ref, mod_ref, chooser_ref, high_ref, low_ref, first_ref, second_ref,
    out_ref, att, norm, slots, keys, vals, halo_send, halo_recv, halo_own,
    tokens, first, second, hidden, part, r1, r2, r3,
    send_sem, token_sem, s1_sem, s2_sem, s3_sem, own_sem,
):
    me, p, y, c, plane_of = positions(n)
    loads = [
        pltpu.make_async_copy(first_ref, first, own_sem.at[1]),
        pltpu.make_async_copy(second_ref, second, own_sem.at[2]),
    ]
    for load in loads:
        load.start()
    targets = [device(p, 1 - y, c), device(p, y, 1 - c)]
    targets += [device(plane, y, c) for plane in plane_of[1:]]
    pending = attention_kernel(
        n, rows, q_ref, k_ref, v_ref, mod_ref, att, norm, keys, vals, halo_send, halo_recv, halo_own,
        also=targets,
    )
    chunk = 512

    def pick(step, carry):
        cols = pl.ds(pl.multiple_of(step * chunk, chunk), chunk)
        slots[:, cols] = jnp.dot(
            chooser_ref[...], norm[:, cols], preferred_element_type=jnp.float32
        ).astype(slots.dtype)
        return carry

    lax.fori_loop(0, D // chunk, pick, 0)
    expert_part(
        n, cap, slots, att, mod_ref, high_ref, low_ref, loads, out_ref,
        tokens, first, second, hidden, part, r1, r2, r3,
        send_sem, token_sem, s1_sem, s2_sem, s3_sem, own_sem,
    )
    for copy, exists in pending:
        when(exists, copy.wait_send)


def expert_part(
    n, cap, slots_ref, att_ref, mod_ref, high_ref, low_ref, weights, out_ref,
    tokens, first, second, hidden, part, r1, r2, r3,
    send_sem, token_sem, s1_sem, s2_sem, s3_sem, own_sem,
):
    planes = n // SPLIT
    width = first.shape[1]
    me, p, y, c, plane_of = positions(n)
    beside = device(p, 1 - y, c)
    twin = device(p, y, 1 - c)

    def block(buf, index):
        return buf.at[pl.ds(pl.multiple_of(index * cap, 16), cap), :]

    mine = pltpu.make_async_copy(block(slots_ref, p), block(tokens, me), own_sem.at[0])
    mine.start()

    sends = []

    def push(src, dst, recv, target):
        copy = remote(src, dst, send_sem.at[len(sends)], recv, target)
        copy.start()
        sends.append(copy)

    def landed(dst, recv):
        remote(dst, dst, send_sem.at[0], recv, me).wait_recv()

    def give(tile, target):
        push(block(tokens, tile), block(tokens, tile), token_sem.at[tile], target)

    def take(tile):
        landed(block(tokens, tile), token_sem.at[tile])

    for target in (beside, twin):
        push(block(slots_ref, p), block(tokens, me), token_sem.at[me], target)
    for plane in plane_of[1:]:
        push(block(slots_ref, plane), block(tokens, me), token_sem.at[me], device(plane, y, c))

    def forward(i, cond=True, copies=None):
        tile = device(plane_of[i], y, c)
        if copies is None:
            copies = []
            for target in (beside, twin):
                ref = block(tokens, tile)
                copies.append(remote(ref, ref, send_sem.at[len(sends)], token_sem.at[tile], target))
                sends.append(copies[-1])

        def go():
            take(tile)
            for copy in copies:
                copy.start()

        when(cond, go)
        return copies

    def forward_more(i):
        tile = device(plane_of[i], 1 - y, c)
        take(tile)
        give(tile, twin)

    group = SPLIT * cap
    chunk = min(width, 256)
    chunk_out = 512

    def compute(i):
        plane = plane_of[i]
        for yy in (0, 1):
            take(device(plane, yy, 1 - c))
        at = pl.ds(pl.multiple_of(plane * group, 16), group)

        def one(step, carry):
            cols = pl.ds(pl.multiple_of(step * chunk, chunk), chunk)
            raw = jnp.dot(tokens[at, :], first[:, cols], preferred_element_type=jnp.float32)
            hidden[:, cols] = jax.nn.gelu(raw, approximate=True).astype(hidden.dtype)
            return carry

        lax.fori_loop(0, width // chunk, one, 0)

        def two(step, carry):
            cols = pl.ds(pl.multiple_of(step * chunk_out, chunk_out), chunk_out)
            raw = jnp.dot(hidden[...], second[:, cols], preferred_element_type=jnp.float32)
            part[at, cols] = raw.astype(part.dtype)
            return carry

        lax.fori_loop(0, D // chunk_out, two, 0)
        for yy in (0, 1):
            push(
                block(part, device(plane, yy, 1 - c)),
                block(r1, plane * 2 + yy),
                s1_sem.at[plane, yy],
                twin,
            )

    def add(tile, other, index):
        def body(step, carry):
            at = pl.ds(pl.multiple_of(tile * cap + step * 16, 16), 16)
            extra = other[pl.ds(pl.multiple_of(index * cap + step * 16, 16), 16), :]
            part[at, :] = (part[at, :].astype(jnp.float32) + extra.astype(jnp.float32)).astype(part.dtype)
            return carry

        lax.fori_loop(0, cap // 16, body, 0)

    def fold_twin(i):
        plane = plane_of[i]
        for yy in (1 - y, y):
            landed(block(r1, plane * 2 + yy), s1_sem.at[plane, yy])
            add(device(plane, yy, c), r1, plane * 2 + yy)
            if yy is not y:
                push(block(part, device(plane, yy, c)), block(r2, plane), s2_sem.at[plane], beside)

    def fold_beside(i):
        plane = plane_of[i]
        landed(block(r2, plane), s2_sem.at[plane])
        tile = device(plane, y, c)
        if i == 0:

            def body(step, carry):
                at = pl.ds(pl.multiple_of(p * cap + step * 16, 16), 16)
                own = part[pl.ds(pl.multiple_of(me * cap + step * 16, 16), 16), :]
                r3[at, :] = (own.astype(jnp.float32) + r2[at, :].astype(jnp.float32)).astype(r3.dtype)
                return carry

            lax.fori_loop(0, cap // 16, body, 0)
        else:
            add(tile, r2, plane)
            push(block(part, tile), block(r3, p), s3_sem.at[p], tile)

    mine.wait()
    take(beside)
    give(beside, twin)
    for load in weights:
        load.wait()
    inner = jnp.logical_and(p > 0, p < planes - 1)
    if planes > 1:
        forward(1)
    if planes > 2:
        early = forward(2, inner)
    compute(0)
    fold_twin(0)
    for i in range(1, planes):
        forward_more(i)
        if i >= 2 and i + 1 < planes:
            forward(i + 1)
        compute(i)
        fold_twin(i)
        fold_beside(i - 1)
        if i == 1 and planes > 2:
            forward(2, jnp.logical_not(inner), early)
    fold_beside(planes - 1)
    for plane in plane_of[1:]:
        landed(block(r3, plane), s3_sem.at[plane])

    def finish(step, carry):
        cols = pl.ds(pl.multiple_of(step * chunk_out, chunk_out), chunk_out)
        found = r3[:, cols]
        mixture = jnp.dot(high_ref[...], found, preferred_element_type=jnp.float32)
        mixture = mixture + jnp.dot(low_ref[...], found, preferred_element_type=jnp.float32)
        out_ref[:, cols] = (
            att_ref[:, cols].astype(jnp.float32) + mod_ref[2:3, cols] * mixture
        ).astype(out_ref.dtype)
        return carry

    lax.fori_loop(0, D // chunk_out, finish, 0)
    for copy in sends:
        copy.wait_send()


def kernel_bytes(n, cap, width):
    planes = n // SPLIT
    lines = 2 * n * cap + planes * 5 * cap + 2 * 3 * halo_levels(n) * cap * planes // 3
    return 2 * (lines * D + 2 * width * D)


def layer(queries, key_rows, values, modulation, expert_in, expert_out, routes, gate_fixed):
    n = lax.axis_size("tile")
    rows = queries.shape[0]
    width = expert_in.shape[1]
    planes = n // SPLIT
    cap = 3 * rows // planes
    flat = routes.reshape(-1)
    target = flat * cap + slot_table(flat, planes)
    target = target.reshape(rows, 2)
    scale = gate_fixed.astype(jnp.float32) / 1024.0
    lines = jnp.arange(planes * cap, dtype=jnp.int32)
    chooser = sum(
        (target[None, :, k] == lines[:, None]).astype(jnp.float32) for k in range(2)
    ).astype(jnp.bfloat16)
    gates = sum(
        jnp.where(target[:, k, None] == lines[None, :], scale[:, k, None], 0.0) for k in range(2)
    )
    coarse = jnp.floor(gates * 128.0) / 128.0
    high = coarse.astype(jnp.bfloat16)
    low = (gates - coarse).astype(jnp.bfloat16)
    levels = halo_levels(n)
    tiles = 3 * levels
    vmem = pl.BlockSpec(memory_space=pltpu.VMEM)
    hbm = pl.BlockSpec(memory_space=pl.ANY)
    dma = pltpu.SemaphoreType.DMA
    count_sends = 8 * planes + 8
    bf = jnp.bfloat16
    return pl.pallas_call(
        functools.partial(layer_kernel, n, rows, cap),
        name="whole_layer",
        out_shape=jax.ShapeDtypeStruct((rows, D), bf),
        in_specs=[vmem, hbm, hbm, vmem, vmem, vmem, vmem, hbm, hbm],
        out_specs=vmem,
        scratch_shapes=[
            pltpu.VMEM((rows, D), bf),
            pltpu.VMEM((rows, D), bf),
            pltpu.VMEM((planes * cap, D), bf),
            pltpu.VMEM((tiles * rows, D), bf),
            pltpu.VMEM((tiles * rows, D), bf),
            dma((4 * (2 + 3 * (levels - 1)),)),
            dma((tiles, 4)),
            dma((2,)),
            pltpu.VMEM((n * cap, D), bf),
            pltpu.VMEM((D, width), bf),
            pltpu.VMEM((width, D), bf),
            pltpu.VMEM((SPLIT * cap, width), bf),
            pltpu.VMEM((n * cap, D), bf),
            pltpu.VMEM((planes * 2 * cap, D), bf),
            pltpu.VMEM((planes * cap, D), bf),
            pltpu.VMEM((planes * cap, D), bf),
            dma((count_sends,)),
            dma((n,)),
            dma((planes, 2)),
            dma((planes,)),
            dma((planes,)),
            dma((3,)),
        ],
        compiler_params=pltpu.CompilerParams(
            collective_id=1, has_side_effects=True, vmem_limit_bytes=VMEM_LIMIT
        ),
    )(queries, key_rows, values, modulation, chooser, high, low, expert_in, expert_out)


def slot_table(flat, experts_count):
    onehot = (flat[:, None] == jnp.arange(experts_count, dtype=jnp.int32)[None, :]).astype(
        jnp.int32
    )
    before = jnp.cumsum(onehot, axis=0) - onehot
    return jnp.sum(before * onehot, axis=1)


def expert_apply(rows, first_weight, second_weight):
    hidden = jax.nn.gelu(
        jnp.dot(rows, first_weight, preferred_element_type=jnp.float32), approximate=True
    ).astype(jnp.bfloat16)
    return jnp.dot(hidden, second_weight, preferred_element_type=jnp.float32).astype(jnp.bfloat16)


def experts_sparse(normed, attended, modulation, expert_in, expert_out, routes, gate_fixed):
    devices = lax.axis_size("tile")
    rows_dev = normed.shape[0]
    experts_count = devices // SPLIT
    capacity = 3 * rows_dev // experts_count
    flat = routes.reshape(-1)
    slots = slot_table(flat, experts_count)
    target = flat * capacity + slots
    chooser = (
        target[None, :] == jnp.arange(experts_count * capacity, dtype=jnp.int32)[:, None]
    ).astype(jnp.bfloat16)
    chooser = chooser.reshape(experts_count * capacity, rows_dev, 2).sum(axis=2)
    buffer = jnp.dot(chooser, normed, preferred_element_type=jnp.float32).astype(jnp.bfloat16)
    copies = jnp.broadcast_to(
        buffer.reshape(experts_count, 1, capacity, D), (experts_count, SPLIT, capacity, D)
    ).reshape(devices, capacity, D)
    received = lax.all_to_all(copies, "tile", split_axis=0, concat_axis=0, tiled=True)
    sources = received.shape[0]
    count = received.shape[1]
    partial_value = expert_apply(received.reshape(sources * count, D), expert_in, expert_out)
    returned = lax.all_to_all(
        partial_value.reshape(sources, count, D), "tile", split_axis=0, concat_axis=0, tiled=True
    )
    summed = jnp.sum(
        returned.reshape(experts_count, SPLIT, capacity, D).astype(jnp.float32), axis=1
    )
    expert_rows = summed.astype(jnp.bfloat16).reshape(experts_count * capacity, D)
    picked = jnp.take(expert_rows, target, axis=0).reshape(rows_dev, 2, D)
    gate_scale = gate_fixed.astype(jnp.float32) / 1024.0
    mixture = jnp.sum(picked.astype(jnp.float32) * gate_scale[:, :, None], axis=1)
    return (attended.astype(jnp.float32) + modulation[2] * mixture).astype(jnp.bfloat16)


def shards(queries, key_rows, values, modulation, expert_in, expert_out, routes, gate_fixed):
    n = lax.axis_size("tile")
    cap = 3 * queries.shape[0] // (n // SPLIT)
    if cap % 16 == 0 and kernel_bytes(n, cap, expert_in.shape[1]) < VMEM_LIMIT * 3 // 4:
        return layer(queries, key_rows, values, modulation, expert_in, expert_out, routes, gate_fixed)
    attended, normed = attention(queries, key_rows, values, modulation)
    return experts_sparse(normed, attended, modulation, expert_in, expert_out, routes, gate_fixed)


def solution(mesh):
    placed = (
        P(("groups", "tile"), None),
        P(("groups", "tile"), None),
        P(("groups", "tile"), None),
        P("groups", None),
        P(None, "tile"),
        P("tile", None),
        P(("groups", "tile"), None),
        P(("groups", "tile"), None),
    )
    return jax.shard_map(
        shards, mesh=mesh, in_specs=placed, out_specs=P(("groups", "tile"), None), check_vma=False
    )
```

profile of v0, /device:TPU:27, one launch (start us, length us, event | category | flops | bytes accessed | tf_op | source)
XLA Modules:
  0.0 178.5 jit_solution(17337482003325182866)
XLA Ops:
  0.0 0.7 convert_multiply_fusion
  0.7 0.8 copy.15
  1.5 0.1 eq.71
  1.6 0.1 fusion.1
  1.7 0.2 reduce_window_sum.11
  1.9 0.2 select_reduce_fusion
  2.0 0.1 reduce_sum.12
  2.2 0.1 copy.16
  2.3 0.7 multiply_add_fusion
  3.0 0.6 add_convert_fusion.chooser_ref
  3.6 0.7 subtract_convert_fusion
  4.3 172.3 %whole_layer.1 = bf16[64,4096]{1,0:T(8,128)(2,1)} custom-call(bf16[64,4096]{1,0:T(8,128)(2,1)} %q_ref.1, bf16[64,4096]{1,0:T(8,128)(2,1)} %k_ref.1, bf16[64,4096]{1,0:T(8,128)(2,1)} %v_ref.1, f32[3,4096]{1,0:T(4,128)} %mod_ref.1, bf16[192,64]{1,0:T(8,128)(2,1)} %add_convert_fusion.chooser_ref, bf16[64,192]{1,0:T(8,128)(2,1)} %get-tuple-element.6.high_ref, ...), custom_call_target="tpu_custom_call" | custom-call | tf_op jit(solution)/shard_map/whole_layer/pallas_call | solution.py:518
  176.6 1.9 %copy.18 = bf16[64,4096]{1,0:T(8,128)(2,1)} copy(bf16[64,4096]{1,0:T(8,128)(2,1)} %whole_layer.1) | data formatting | bytes 1048576
  (2 shorter events, 0.0 us)
where the time goes:
time: 179 us; the launch traced here: 178 us
  Pallas kernels  172 us (96%)
  other arithmetic  3.19 us (2%)
  local copies, waits for them, and re-layouts  3 us (2%)
    pallas_call x1, Pallas kernels, layer(): pl.pallas_call(functools.partial(layer_kernel, n, rows, cap), name='whole...  172 us

commit v1 on v0

--- a/solution.py
+++ b/solution.py
@@ -54,7 +54,6 @@
 
 def attention_kernel(
     n, rows, q_ref, k_ref, v_ref, mod_ref, att_ref, norm_ref, keys, vals, send_sem, recv_sem, own_sem,
-    also=None,
 ):
     me = lax.axis_index("tile")
     grid_rows = n // TILE_COLS
@@ -106,7 +105,6 @@
     barrier = pltpu.get_barrier_semaphore()
     partners = [(over(offset), exists) for _, offset, exists, _ in verticals]
     partners += [(beside(side), exists) for side, exists in sides]
-    partners += [(target, True) for target in also or []]
     for target, exists in partners:
 
         def greet(target=target):
@@ -219,8 +217,6 @@
         return carry
 
     lax.fori_loop(0, rows // 16, normalise, 0)
-    if also is not None:
-        return sends
     for copy, exists in sends:
         when(exists, copy.wait_send)
 
@@ -254,237 +250,509 @@
     )(queries, key_rows, values, modulation)
 
 
-def nearest_first(p, planes):
-    order = [p] + [p * 0] * (planes - 1)
-    count = p * 0 + 1
-    for step in range(1, planes):
-        for other in (p - step, p + step):
-            exists = jnp.logical_and(other >= 0, other < planes)
-            for i in range(1, planes):
-                order[i] = jnp.where(jnp.logical_and(exists, count == i), other, order[i])
-            count = count + jnp.where(exists, 1, 0)
-    return order
-
-
-def positions(n):
+def device(plane, yy, cc):
+    return plane * SPLIT + yy * 2 + cc
+
+
+def layer_kernel(
+    n, rows, cap, chunks, q_ref, k_ref, v_ref, mod_ref, routes_ref, gates_ref, first_ref, second_ref,
+    out_ref, att, bias, keys, vals, line, tokens, stage, chooser, tables, stats, normed, first, second,
+    hidden, part, r1, r2, pair, acc_in, acc_out,
+    own_sem, kv_send, kv_recv, table_send, table_recv, stat_send, stat_recv, out_send, line_recv,
+    token_recv, back_send, s1_recv, s2_recv, pair_recv, acc_recv,
+):
+    planes = n // SPLIT
+    width = first.shape[1]
+    wide = D // chunks
     me = lax.axis_index("tile")
     p = lax.div(me, SPLIT)
-    q = lax.rem(me, SPLIT)
-    return me, p, lax.div(q, 2), lax.rem(q, 2), nearest_first(p, n // SPLIT)
-
-
-def device(plane, yy, cc):
-    return plane * SPLIT + yy * 2 + cc
-
-
-def layer_kernel(
-    n, rows, cap, q_ref, k_ref, v_ref, mod_ref, chooser_ref, high_ref, low_ref, first_ref, second_ref,
-    out_ref, att, norm, slots, keys, vals, halo_send, halo_recv, halo_own,
-    tokens, first, second, hidden, part, r1, r2, r3,
-    send_sem, token_sem, s1_sem, s2_sem, s3_sem, own_sem,
-):
-    me, p, y, c, plane_of = positions(n)
+    y = lax.div(lax.rem(me, SPLIT), 2)
+    c = lax.rem(me, 2)
+    beside = device(p, 1 - y, c)
+    twin = device(p, y, 1 - c)
+    low_half = p < planes // 2
+    toward = jnp.where(low_half, 1, -1)
+    inner = p + toward
+    outer = p - toward
+    at_end = jnp.logical_or(p == 0, p == planes - 1)
+    middle = jnp.logical_not(at_end)
+    outer_expert = jnp.where(low_half, 0, planes - 1)
+    inner_device = device(inner, y, c)
+    outer_device = device(jnp.where(at_end, p, outer), y, c)
+
+    tile = lax.rem(me + TILE_COLS // 2, n)
+    column = lax.rem(tile, TILE_COLS)
+    partner = lax.rem(me + TILE_COLS, n)
+    sides = [(-1, column > 0), (1, column < TILE_COLS - 1)]
+    half_way = TILE_COLS // 2
+    crossing = {-1: column == half_way, 1: column == half_way - 1}
+
+    def cols(j):
+        return pl.ds(pl.multiple_of(j * wide, wide), wide)
+
+    def lines(buf, s):
+        return buf.at[pl.ds(pl.multiple_of(s * rows, rows), rows), :]
+
     loads = [
-        pltpu.make_async_copy(first_ref, first, own_sem.at[1]),
-        pltpu.make_async_copy(second_ref, second, own_sem.at[2]),
+        pltpu.make_async_copy(k_ref, lines(keys, 1), own_sem.at[0]),
+        pltpu.make_async_copy(v_ref, lines(vals, 1), own_sem.at[1]),
+        pltpu.make_async_copy(first_ref, first, own_sem.at[2]),
+        pltpu.make_async_copy(second_ref, second, own_sem.at[3]),
     ]
     for load in loads:
         load.start()
-    targets = [device(p, 1 - y, c), device(p, y, 1 - c)]
-    targets += [device(plane, y, c) for plane in plane_of[1:]]
-    pending = attention_kernel(
-        n, rows, q_ref, k_ref, v_ref, mod_ref, att, norm, keys, vals, halo_send, halo_recv, halo_own,
-        also=targets,
+
+    barrier = pltpu.get_barrier_semaphore()
+    others = [lax.rem(me + step, n) for step in range(1, n)]
+    for target in others:
+        pl.semaphore_signal(barrier, inc=1, device_id={"tile": target}, device_id_type=MESH)
+    pl.semaphore_wait(barrier, n - 1)
+
+    def beside_tile(side):
+        return lax.rem(me + side + jnp.where(crossing[side], TILE_COLS, 0) + n, n)
+
+    def slot_there(level, side):
+        return jnp.where(crossing[side], 1 - level, level) * 3 + 1 - side
+
+    bufs = (keys, vals)
+
+    def place(i, s, j):
+        return bufs[i].at[pl.ds(pl.multiple_of(s * rows, rows), rows), cols(j)]
+
+    def over_vertical(i, j):
+        return remote(
+            (k_ref, v_ref)[i].at[:, cols(j)], place(i, 4, j), kv_send.at[i, j], kv_recv.at[8 + i, j], partner
+        )
+
+    def over_side(level, index, i, j):
+        side = sides[index][0]
+        there = slot_there(level, side)
+        source = (k_ref, v_ref)[i].at[:, cols(j)] if level == 0 else place(i, 4, j)
+        return remote(
+            source,
+            place(i, there, j),
+            kv_send.at[2 + level * 4 + index * 2 + i, j],
+            kv_recv.at[there * 2 + i, j],
+            beside_tile(side),
+        )
+
+    def landed(ref, sem):
+        remote(ref, ref, own_sem.at[0], sem, me).wait_recv()
+
+    def send_own(j):
+        for i in (0, 1):
+            over_vertical(i, j).start()
+        for i in (0, 1):
+            for index, (_, exists) in enumerate(sides):
+                when(exists, over_side(0, index, i, j).start)
+
+    def send_vertical(j):
+        for i in (0, 1):
+            landed(place(i, 4, j), kv_recv.at[8 + i, j])
+            for index, (_, exists) in enumerate(sides):
+                when(exists, over_side(1, index, i, j).start)
+
+    for j in range(min(2, chunks)):
+        send_own(j)
+
+    expert = lax.broadcasted_iota(jnp.int32, (8, rows), 0)
+    named = [routes_ref[k : k + 1, :] == expert for k in (0, 1)]
+    member = jnp.logical_or(named[0], named[1])
+    upto = (
+        lax.broadcasted_iota(jnp.int32, (rows, rows), 0) <= lax.broadcasted_iota(jnp.int32, (rows, rows), 1)
+    ).astype(jnp.float32).astype(jnp.bfloat16)
+    count = jnp.dot(
+        member.astype(jnp.float32).astype(jnp.bfloat16), upto, preferred_element_type=jnp.float32
     )
-    chunk = 512
-
-    def pick(step, carry):
-        cols = pl.ds(pl.multiple_of(step * chunk, chunk), chunk)
-        slots[:, cols] = jnp.dot(
-            chooser_ref[...], norm[:, cols], preferred_element_type=jnp.float32
-        ).astype(slots.dtype)
+    gate = sum(
+        jnp.where(named[k], gates_ref[k : k + 1, :].astype(jnp.float32), 0.0) for k in (0, 1)
+    )
+    tables[me, 0:8, :] = jnp.where(member, count - 1.0, -1.0)
+    tables[me, 8:16, :] = gate / 1024.0
+
+    def tell(ref, send, recv):
+        return [
+            remote(ref.at[me], ref.at[me], send.at[step], recv.at[me], target)
+            for step, target in enumerate(others)
+        ]
+
+    for copy in tell(tables, table_send, table_recv):
+        copy.start()
+
+    span = 6 * rows
+    where = lax.broadcasted_iota(jnp.int32, (rows, span), 1)
+    penalty = jnp.zeros((rows, span), jnp.float32)
+    for s in range(6):
+        for side, exists in sides:
+            if side != s % 3 - 1:
+                continue
+            here = (where >= s * rows) & (where < (s + 1) * rows)
+            penalty = jnp.where(here, jnp.where(exists, 0.0, MASKED), penalty)
+
+            def clear(s=s):
+                for buf in bufs:
+                    buf[s * rows : (s + 1) * rows, :] = jnp.zeros((rows, D), buf.dtype)
+
+            pl.when(jnp.logical_not(exists))(clear)
+    bias[...] = penalty
+    for load in loads[:2]:
+        load.wait()
+    for target in others:
+        landed(tables.at[target], table_recv.at[target])
+
+    slot_line = lax.broadcasted_iota(jnp.int32, (cap, rows), 0).astype(jnp.float32)
+
+    def chosen(tile_there, e):
+        return tables[tile_there, pl.ds(e, 1), :] == slot_line
+
+    for plane in range(planes):
+        for place_in, e in ((0, p), (1, outer_expert)):
+            chooser[plane, place_in * cap : (place_in + 1) * cap, :] = (
+                chosen(device(plane, y, c), e).astype(jnp.float32).astype(jnp.bfloat16)
+            )
+
+    scale = 1.0 / math.sqrt(HEAD_DIM)
+
+    def attend(j):
+        for level in (0, 1):
+            for side, exists in sides:
+                s = level * 3 + 1 + side
+                for i in (0, 1):
+                    when(exists, functools.partial(landed, place(i, s, j), kv_recv.at[s * 2 + i, j]))
+        for extra in range(wide // HEAD_DIM):
+            at = pl.ds(pl.multiple_of(j * wide + extra * HEAD_DIM, HEAD_DIM), HEAD_DIM)
+            scores = lax.dot_general(
+                q_ref[:, at], keys[:, at], (((1,), (1,)), ((), ())), preferred_element_type=jnp.float32
+            )
+            scores = scores * scale + bias[...]
+            raised = jnp.exp(scores - jnp.max(scores, axis=-1, keepdims=True))
+            probs = (raised * (1.0 / jnp.sum(raised, axis=-1, keepdims=True))).astype(jnp.bfloat16)
+            att[:, at] = jnp.dot(probs, vals[:, at], preferred_element_type=jnp.float32).astype(att.dtype)
+
+    def raw_copy(k, src, j):
+        source = att.at[:, cols(j)] if k == 0 else line.at[src, :, cols(j)]
+        return remote(source, line.at[src, :, cols(j)], out_send.at[k, 0, j], line_recv.at[src, j], inner_device)
+
+    def outer_copy(k, src, j):
+        there = device(src, y, c)
+        return remote(
+            stage.at[src, :, cols(j)],
+            tokens.at[there, :, cols(j)],
+            out_send.at[k, 1, j],
+            token_recv.at[there, j],
+            outer_device,
+        )
+
+    def plane_copy(k, src, j, index):
+        ref = tokens.at[device(src, y, c), :, cols(j)]
+        return remote(
+            ref, ref, out_send.at[k, 2 + index, j], token_recv.at[device(src, y, c), j], (beside, twin)[index]
+        )
+
+    def twin_copy(k, src, j):
+        there = device(src, 1 - y, c)
+        ref = tokens.at[there, :, cols(j)]
+        return remote(ref, ref, out_send.at[k, 4, j], token_recv.at[there, j], twin)
+
+    far = jnp.where(at_end, p + 3 * toward, p + 2 * toward)
+    second_plane = jnp.where(at_end, p + 2 * toward, outer)
+    sources = [
+        (p, 1, True, middle),
+        (inner, 2, False, middle),
+        (second_plane, jnp.where(at_end, 3, 2), middle, False),
+        (far, jnp.where(at_end, 4, 3), False, middle),
+    ]
+
+    def relay(k, j):
+        src, behind, whole, out = sources[k]
+        jj = j - behind
+
+        def go():
+            there = device(src, y, c)
+            if k > 0:
+                pl.when(at_end)(
+                    lambda: landed(tokens.at[there, :, cols(jj)], token_recv.at[there, jj])
+                )
+                pl.when(middle)(lambda: landed(line.at[src, :, cols(jj)], line_recv.at[src, jj]))
+            if whole is not False:
+                when(whole, raw_copy(k, src, jj).start)
+
+            def pick():
+                rows_here = att[:, cols(jj)] if k == 0 else line[src, :, cols(jj)]
+                picked = jnp.dot(chooser[src], rows_here, preferred_element_type=jnp.float32).astype(
+                    tokens.dtype
+                )
+                tokens[there, :, cols(jj)] = picked[:cap]
+                stage[src, :, cols(jj)] = picked[cap:]
+
+            when(True if k == 0 else middle, pick)
+            if out is not False:
+                when(out, outer_copy(k, src, jj).start)
+            for index in (0, 1):
+                plane_copy(k, src, jj, index).start()
+
+        pl.when(jnp.logical_and(jj >= 0, jj < chunks))(go)
+
+    def pass_on(k, j):
+        src, behind, _, _ = sources[k]
+        jj = j - behind - 1
+
+        def go():
+            there = device(src, 1 - y, c)
+            landed(tokens.at[there, :, cols(jj)], token_recv.at[there, jj])
+            twin_copy(k, src, jj).start()
+
+        pl.when(jnp.logical_and(jj >= 0, jj < chunks))(go)
+
+    def move(j):
+        for k in range(planes):
+            relay(k, j)
+        for k in range(planes):
+            pass_on(k, j)
+
+    def stream(j, carry):
+        pl.when(j + 2 < chunks)(lambda: send_own(j + 2))
+        pl.when(j < chunks)(lambda: send_vertical(j))
+        pl.when(j >= 1)(lambda: attend(j - 1))
+        move(j)
         return carry
 
-    lax.fori_loop(0, D // chunk, pick, 0)
-    expert_part(
-        n, cap, slots, att, mod_ref, high_ref, low_ref, loads, out_ref,
-        tokens, first, second, hidden, part, r1, r2, r3,
-        send_sem, token_sem, s1_sem, s2_sem, s3_sem, own_sem,
-    )
-    for copy, exists in pending:
-        when(exists, copy.wait_send)
-
-
-def expert_part(
-    n, cap, slots_ref, att_ref, mod_ref, high_ref, low_ref, weights, out_ref,
-    tokens, first, second, hidden, part, r1, r2, r3,
-    send_sem, token_sem, s1_sem, s2_sem, s3_sem, own_sem,
-):
-    planes = n // SPLIT
-    width = first.shape[1]
-    me, p, y, c, plane_of = positions(n)
-    beside = device(p, 1 - y, c)
-    twin = device(p, y, 1 - c)
-
-    def block(buf, index):
-        return buf.at[pl.ds(pl.multiple_of(index * cap, 16), cap), :]
-
-    mine = pltpu.make_async_copy(block(slots_ref, p), block(tokens, me), own_sem.at[0])
-    mine.start()
-
-    sends = []
-
-    def push(src, dst, recv, target):
-        copy = remote(src, dst, send_sem.at[len(sends)], recv, target)
+    lax.fori_loop(0, chunks + 1, stream, 0)
+
+    token = lax.broadcasted_iota(jnp.int32, (16, rows), 1)
+    line_of = lax.broadcasted_iota(jnp.int32, (16, rows), 0)
+    mean_row = jnp.zeros((1, rows), jnp.float32)
+    rate_row = jnp.zeros((1, rows), jnp.float32)
+    for step in range(rows // 16):
+        some = att[step * 16 : (step + 1) * 16, :].astype(jnp.float32)
+        mean = jnp.mean(some, axis=-1, keepdims=True)
+        some = some - mean
+        rate = lax.rsqrt(jnp.mean(some * some, axis=-1, keepdims=True) + EPSILON)
+        same = token == line_of + step * 16
+        mean_row = mean_row + jnp.sum(jnp.where(same, mean, 0.0), axis=0, keepdims=True)
+        rate_row = rate_row + jnp.sum(jnp.where(same, rate, 0.0), axis=0, keepdims=True)
+    stats[me] = jnp.where(lax.broadcasted_iota(jnp.int32, (8, rows), 0) == 0, mean_row, rate_row)
+    for copy in tell(stats, stat_send, stat_recv):
         copy.start()
-        sends.append(copy)
-
-    def landed(dst, recv):
-        remote(dst, dst, send_sem.at[0], recv, me).wait_recv()
-
-    def give(tile, target):
-        push(block(tokens, tile), block(tokens, tile), token_sem.at[tile], target)
-
-    def take(tile):
-        landed(block(tokens, tile), token_sem.at[tile])
-
-    for target in (beside, twin):
-        push(block(slots_ref, p), block(tokens, me), token_sem.at[me], target)
-    for plane in plane_of[1:]:
-        push(block(slots_ref, plane), block(tokens, me), token_sem.at[me], device(plane, y, c))
-
-    def forward(i, cond=True, copies=None):
-        tile = device(plane_of[i], y, c)
-        if copies is None:
-            copies = []
-            for target in (beside, twin):
-                ref = block(tokens, tile)
-                copies.append(remote(ref, ref, send_sem.at[len(sends)], token_sem.at[tile], target))
-                sends.append(copies[-1])
-
-        def go():
-            take(tile)
-            for copy in copies:
-                copy.start()
-
-        when(cond, go)
-        return copies
-
-    def forward_more(i):
-        tile = device(plane_of[i], 1 - y, c)
-        take(tile)
-        give(tile, twin)
-
+
+    def drain(j, carry):
+        move(j)
+        return carry
+
+    lax.fori_loop(chunks + 1, chunks + 5, drain, 0)
+    for target in others:
+        landed(stats.at[target], stat_recv.at[target])
+    for load in loads[2:]:
+        load.wait()
+
+    order = [
+        jnp.where(at_end, p + 3 * toward, p + 2 * toward),
+        jnp.where(at_end, p + 2 * toward, inner),
+        jnp.where(at_end, inner, outer),
+        p,
+    ]
     group = SPLIT * cap
     chunk = min(width, 256)
     chunk_out = 512
 
+    def block(buf, index):
+        return buf.at[pl.ds(pl.multiple_of(index * cap, 16), cap), :]
+
+    def picked_column(tile_there, row):
+        return jnp.sum(jnp.where(chosen(tile_there, p), row, 0.0), axis=1, keepdims=True)
+
     def compute(i):
-        plane = plane_of[i]
-        for yy in (0, 1):
-            take(device(plane, yy, 1 - c))
-        at = pl.ds(pl.multiple_of(plane * group, 16), group)
+        plane = order[i]
+
+        def arrive(j, carry):
+            for yy in (0, 1):
+                there = device(plane, yy, 1 - c)
+                landed(tokens.at[there, :, cols(j)], token_recv.at[there, j])
+            return carry
+
+        lax.fori_loop(0, chunks, arrive, 0)
+
+        def normalise(t, carry):
+            there = plane * SPLIT + t
+            mean = picked_column(there, stats[there, 0:1, :])
+            rate = picked_column(there, stats[there, 1:2, :])
+            at = pl.ds(pl.multiple_of(t * cap, 16), cap)
+            for step in range(D // chunk_out):
+                some = slice(step * chunk_out, (step + 1) * chunk_out)
+                value = (tokens[there, :, some].astype(jnp.float32) - mean) * rate
+                normed[at, some] = (value * (1.0 + mod_ref[1:2, some]) + mod_ref[0:1, some]).astype(
+                    normed.dtype
+                )
+            return carry
+
+        lax.fori_loop(0, SPLIT, normalise, 0)
 
         def one(step, carry):
-            cols = pl.ds(pl.multiple_of(step * chunk, chunk), chunk)
-            raw = jnp.dot(tokens[at, :], first[:, cols], preferred_element_type=jnp.float32)
-            hidden[:, cols] = jax.nn.gelu(raw, approximate=True).astype(hidden.dtype)
+            at = pl.ds(pl.multiple_of(step * chunk, chunk), chunk)
+            raw = jnp.dot(normed[...], first[:, at], preferred_element_type=jnp.float32)
+            hidden[:, at] = jax.nn.gelu(raw, approximate=True).astype(hidden.dtype)
             return carry
 
         lax.fori_loop(0, width // chunk, one, 0)
+        mine = pl.ds(pl.multiple_of(plane * group, 16), group)
 
         def two(step, carry):
-            cols = pl.ds(pl.multiple_of(step * chunk_out, chunk_out), chunk_out)
-            raw = jnp.dot(hidden[...], second[:, cols], preferred_element_type=jnp.float32)
-            part[at, cols] = raw.astype(part.dtype)
+            at = pl.ds(pl.multiple_of(step * chunk_out, chunk_out), chunk_out)
+            raw = jnp.dot(hidden[...], second[:, at], preferred_element_type=jnp.float32)
+            part[mine, at] = raw.astype(part.dtype)
             return carry
 
         lax.fori_loop(0, D // chunk_out, two, 0)
         for yy in (0, 1):
-            push(
-                block(part, device(plane, yy, 1 - c)),
-                block(r1, plane * 2 + yy),
-                s1_sem.at[plane, yy],
-                twin,
-            )
-
-    def add(tile, other, index):
-        def body(step, carry):
-            at = pl.ds(pl.multiple_of(tile * cap + step * 16, 16), 16)
-            extra = other[pl.ds(pl.multiple_of(index * cap + step * 16, 16), 16), :]
-            part[at, :] = (part[at, :].astype(jnp.float32) + extra.astype(jnp.float32)).astype(part.dtype)
-            return carry
-
-        lax.fori_loop(0, cap // 16, body, 0)
+            to_twin(i, yy).start()
+
+    def to_twin(i, yy):
+        plane = order[i]
+        return remote(
+            block(part, device(plane, yy, 1 - c)),
+            block(r1, plane * 2 + yy),
+            back_send.at[i, yy],
+            s1_recv.at[plane, yy],
+            twin,
+        )
+
+    def to_beside(i):
+        plane = order[i]
+        return remote(
+            block(part, device(plane, 1 - y, c)), block(r2, plane), back_send.at[i, 2], s2_recv.at[plane], beside
+        )
 
     def fold_twin(i):
-        plane = plane_of[i]
+        plane = order[i]
         for yy in (1 - y, y):
-            landed(block(r1, plane * 2 + yy), s1_sem.at[plane, yy])
-            add(device(plane, yy, c), r1, plane * 2 + yy)
+            landed(block(r1, plane * 2 + yy), s1_recv.at[plane, yy])
+            base = device(plane, yy, c) * cap
+            from_there = (plane * 2 + yy) * cap
+
+            def body(step, carry):
+                at = pl.ds(pl.multiple_of(base + step * 16, 16), 16)
+                extra = r1[pl.ds(pl.multiple_of(from_there + step * 16, 16), 16), :]
+                part[at, :] = (part[at, :].astype(jnp.float32) + extra.astype(jnp.float32)).astype(part.dtype)
+                return carry
+
+            lax.fori_loop(0, cap // 16, body, 0)
             if yy is not y:
-                push(block(part, device(plane, yy, c)), block(r2, plane), s2_sem.at[plane], beside)
+                to_beside(i).start()
 
     def fold_beside(i):
-        plane = plane_of[i]
-        landed(block(r2, plane), s2_sem.at[plane])
-        tile = device(plane, y, c)
-        if i == 0:
+        plane = order[i]
+        there = device(plane, y, c)
+        landed(block(r2, plane), s2_recv.at[plane])
+        weight = picked_column(there, tables[there, pl.ds(8 + p, 1), :])
+        ours = pl.ds(pl.multiple_of(there * cap, 16), cap)
+        theirs = pl.ds(pl.multiple_of(plane * cap, 16), cap)
+        for step in range(D // chunk_out):
+            some = slice(step * chunk_out, (step + 1) * chunk_out)
+            total = part[ours, some].astype(jnp.float32) + r2[theirs, some].astype(jnp.float32)
+            pair[plane, :cap, some] = (total * weight).astype(pair.dtype)
+
+    def slots_home(i):
+        plane = order[i]
+        return remote(
+            pair.at[plane, pl.ds(0, cap), :],
+            pair.at[plane, pl.ds(cap, cap), :],
+            back_send.at[i, 3],
+            pair_recv.at[plane],
+            inner_device,
+        )
+
+    def rows_home(i):
+        plane = order[i]
+        return remote(
+            acc_out.at[plane],
+            acc_in.at[plane],
+            back_send.at[i, 3],
+            acc_recv.at[plane],
+            outer_device if i == 2 else inner_device,
+        )
+
+    def spread_out(plane, both, at):
+        amount = 2 * cap if both else cap
+        return lax.dot_general(
+            chooser[plane, :amount, :],
+            pair[plane, :amount, at],
+            (((0,), (0,)), ((), ())),
+            preferred_element_type=jnp.float32,
+        )
+
+    def fold_home(i):
+        plane = order[i]
+
+        def fold(both, extra, last):
+            if both:
+                landed(pair.at[plane, pl.ds(cap, cap), :], pair_recv.at[plane])
+            if extra:
+                landed(acc_in.at[plane], acc_recv.at[plane])
 
             def body(step, carry):
-                at = pl.ds(pl.multiple_of(p * cap + step * 16, 16), 16)
-                own = part[pl.ds(pl.multiple_of(me * cap + step * 16, 16), 16), :]
-                r3[at, :] = (own.astype(jnp.float32) + r2[at, :].astype(jnp.float32)).astype(r3.dtype)
+                at = pl.ds(pl.multiple_of(step * chunk_out, chunk_out), chunk_out)
+                total = spread_out(plane, both, at)
+                if extra:
+                    total = total + acc_in[plane, :, at].astype(jnp.float32)
+                if last:
+                    out_ref[:, at] = (att[:, at].astype(jnp.float32) + mod_ref[2:3, at] * total).astype(
+                        out_ref.dtype
+                    )
+                else:
+                    acc_out[plane, :, at] = total.astype(acc_out.dtype)
                 return carry
 
-            lax.fori_loop(0, cap // 16, body, 0)
+            lax.fori_loop(0, D // chunk_out, body, 0)
+            if not last:
+                rows_home(i).start()
+
+        if i == 3:
+            pl.when(at_end)(lambda: fold(False, True, True))
+            pl.when(middle)(lambda: fold(True, True, True))
         else:
-            add(tile, r2, plane)
-            push(block(part, tile), block(r3, p), s3_sem.at[p], tile)
-
-    mine.wait()
-    take(beside)
-    give(beside, twin)
-    for load in weights:
-        load.wait()
-    inner = jnp.logical_and(p > 0, p < planes - 1)
-    if planes > 1:
-        forward(1)
-    if planes > 2:
-        early = forward(2, inner)
-    compute(0)
-    fold_twin(0)
-    for i in range(1, planes):
-        forward_more(i)
-        if i >= 2 and i + 1 < planes:
-            forward(i + 1)
+            pl.when(at_end)(slots_home(i).start)
+            pl.when(middle)(lambda: fold(i < 2, i == 2, False))
+
+    for i in range(planes):
         compute(i)
         fold_twin(i)
-        fold_beside(i - 1)
-        if i == 1 and planes > 2:
-            forward(2, jnp.logical_not(inner), early)
+        if i > 0:
+            fold_beside(i - 1)
+            fold_home(i - 1)
     fold_beside(planes - 1)
-    for plane in plane_of[1:]:
-        landed(block(r3, plane), s3_sem.at[plane])
-
-    def finish(step, carry):
-        cols = pl.ds(pl.multiple_of(step * chunk_out, chunk_out), chunk_out)
-        found = r3[:, cols]
-        mixture = jnp.dot(high_ref[...], found, preferred_element_type=jnp.float32)
-        mixture = mixture + jnp.dot(low_ref[...], found, preferred_element_type=jnp.float32)
-        out_ref[:, cols] = (
-            att_ref[:, cols].astype(jnp.float32) + mod_ref[2:3, cols] * mixture
-        ).astype(out_ref.dtype)
+    fold_home(planes - 1)
+
+    def left(j, carry):
+        for i in (0, 1):
+            over_vertical(i, j).wait_send()
+            for level in (0, 1):
+                for index, (_, exists) in enumerate(sides):
+                    when(exists, over_side(level, index, i, j).wait_send)
+        for k, (src, _, whole, out) in enumerate(sources):
+            if whole is not False:
+                when(whole, raw_copy(k, src, j).wait_send)
+            if out is not False:
+                when(out, outer_copy(k, src, j).wait_send)
+            for index in (0, 1):
+                plane_copy(k, src, j, index).wait_send()
+            twin_copy(k, src, j).wait_send()
         return carry
 
-    lax.fori_loop(0, D // chunk_out, finish, 0)
-    for copy in sends:
+    lax.fori_loop(0, chunks, left, 0)
+    for copy in tell(tables, table_send, table_recv) + tell(stats, stat_send, stat_recv):
         copy.wait_send()
-
-
-def kernel_bytes(n, cap, width):
+    for i in range(planes):
+        for yy in (0, 1):
+            to_twin(i, yy).wait_send()
+        to_beside(i).wait_send()
+        if i < planes - 1:
+            pl.when(at_end)(slots_home(i).wait_send)
+            pl.when(middle)(rows_home(i).wait_send)
+
+
+def kernel_bytes(n, rows, cap, width):
     planes = n // SPLIT
-    lines = 2 * n * cap + planes * 5 * cap + 2 * 3 * halo_levels(n) * cap * planes // 3
+    lines = 2 * 6 * rows + 2 * n * cap + planes * (6 * cap + 3 * rows) + SPLIT * cap + 3 * rows
     return 2 * (lines * D + 2 * width * D)
 
 
@@ -494,61 +762,58 @@
     width = expert_in.shape[1]
     planes = n // SPLIT
     cap = 3 * rows // planes
-    flat = routes.reshape(-1)
-    target = flat * cap + slot_table(flat, planes)
-    target = target.reshape(rows, 2)
-    scale = gate_fixed.astype(jnp.float32) / 1024.0
-    lines = jnp.arange(planes * cap, dtype=jnp.int32)
-    chooser = sum(
-        (target[None, :, k] == lines[:, None]).astype(jnp.float32) for k in range(2)
-    ).astype(jnp.bfloat16)
-    gates = sum(
-        jnp.where(target[:, k, None] == lines[None, :], scale[:, k, None], 0.0) for k in range(2)
-    )
-    coarse = jnp.floor(gates * 128.0) / 128.0
-    high = coarse.astype(jnp.bfloat16)
-    low = (gates - coarse).astype(jnp.bfloat16)
-    levels = halo_levels(n)
-    tiles = 3 * levels
+    chunks = 8
     vmem = pl.BlockSpec(memory_space=pltpu.VMEM)
     hbm = pl.BlockSpec(memory_space=pl.ANY)
     dma = pltpu.SemaphoreType.DMA
-    count_sends = 8 * planes + 8
     bf = jnp.bfloat16
     return pl.pallas_call(
-        functools.partial(layer_kernel, n, rows, cap),
+        functools.partial(layer_kernel, n, rows, cap, chunks),
         name="whole_layer",
         out_shape=jax.ShapeDtypeStruct((rows, D), bf),
-        in_specs=[vmem, hbm, hbm, vmem, vmem, vmem, vmem, hbm, hbm],
+        in_specs=[vmem, hbm, hbm, vmem, vmem, vmem, hbm, hbm],
         out_specs=vmem,
         scratch_shapes=[
             pltpu.VMEM((rows, D), bf),
-            pltpu.VMEM((rows, D), bf),
-            pltpu.VMEM((planes * cap, D), bf),
-            pltpu.VMEM((tiles * rows, D), bf),
-            pltpu.VMEM((tiles * rows, D), bf),
-            dma((4 * (2 + 3 * (levels - 1)),)),
-            dma((tiles, 4)),
-            dma((2,)),
-            pltpu.VMEM((n * cap, D), bf),
+            pltpu.VMEM((rows, 6 * rows), jnp.float32),
+            pltpu.VMEM((6 * rows, D), bf),
+            pltpu.VMEM((6 * rows, D), bf),
+            pltpu.VMEM((planes, rows, D), bf),
+            pltpu.VMEM((n, cap, D), bf),
+            pltpu.VMEM((planes, cap, D), bf),
+            pltpu.VMEM((planes, 2 * cap, rows), bf),
+            pltpu.VMEM((n, 16, rows), jnp.float32),
+            pltpu.VMEM((n, 8, rows), jnp.float32),
+            pltpu.VMEM((SPLIT * cap, D), bf),
             pltpu.VMEM((D, width), bf),
             pltpu.VMEM((width, D), bf),
             pltpu.VMEM((SPLIT * cap, width), bf),
             pltpu.VMEM((n * cap, D), bf),
             pltpu.VMEM((planes * 2 * cap, D), bf),
             pltpu.VMEM((planes * cap, D), bf),
-            pltpu.VMEM((planes * cap, D), bf),
-            dma((count_sends,)),
+            pltpu.VMEM((planes, 2 * cap, D), bf),
+            pltpu.VMEM((planes, rows, D), bf),
+            pltpu.VMEM((planes, rows, D), bf),
+            dma((4,)),
+            dma((10, chunks)),
+            dma((12, chunks)),
+            dma((n - 1,)),
             dma((n,)),
+            dma((n - 1,)),
+            dma((n,)),
+            dma((planes, 5, chunks)),
+            dma((planes, chunks)),
+            dma((n, chunks)),
+            dma((planes, 4)),
             dma((planes, 2)),
             dma((planes,)),
             dma((planes,)),
-            dma((3,)),
+            dma((planes,)),
         ],
         compiler_params=pltpu.CompilerParams(
             collective_id=1, has_side_effects=True, vmem_limit_bytes=VMEM_LIMIT
         ),
-    )(queries, key_rows, values, modulation, chooser, high, low, expert_in, expert_out)
+    )(queries, key_rows, values, modulation, routes.T, gate_fixed.T, expert_in, expert_out)
 
 
 def slot_table(flat, experts_count):
@@ -602,7 +867,7 @@
 def shards(queries, key_rows, values, modulation, expert_in, expert_out, routes, gate_fixed):
     n = lax.axis_size("tile")
     cap = 3 * queries.shape[0] // (n // SPLIT)
-    if cap % 16 == 0 and kernel_bytes(n, cap, expert_in.shape[1]) < VMEM_LIMIT * 3 // 4:
+    if n == 2 * TILE_COLS and cap % 16 == 0 and kernel_bytes(n, queries.shape[0], cap, expert_in.shape[1]) < VMEM_LIMIT * 7 // 8:
         return layer(queries, key_rows, values, modulation, expert_in, expert_out, routes, gate_fixed)
     attended, normed = attention(queries, key_rows, values, modulation)
     return experts_sparse(normed, attended, modulation, expert_in, expert_out, routes, gate_fixed)

time: 179 us -> 172 us (0.961)
  the two profiles are of different devices: /device:TPU:27 before, /device:TPU:0 now
where the time goes in v1:
time: 172 us
  Pallas kernels  170 us (99%)
  local copies, waits for them, and re-layouts  1.87 us (1%)
    pallas_call x1, Pallas kernels, layer(): pl.pallas_call(functools.partial(layer_kernel, n, rows, cap, chunks), nam...  170 us

profile of v1, /device:TPU:0, one launch (start us, length us, event | category | flops | bytes accessed | tf_op | source)
XLA Modules:
  0.0 171.8 jit_solution(18135948498650216351)
XLA Ops:
  0.0 169.9 %whole_layer.1 = bf16[64,4096]{1,0:T(8,128)(2,1)} custom-call(bf16[64,4096]{1,0:T(8,128)(2,1)} %q_ref.1, bf16[64,4096]{1,0:T(8,128)(2,1)} %k_ref.1, bf16[64,4096]{1,0:T(8,128)(2,1)} %v_ref.1, f32[3,4096]{1,0:T(4,128)} %mod_ref.1, s32[2,64]{1,0:T(2,128)} %bitcast.2, s32[2,64]{1,0:T(2,128)} %bitcast.3, bf16[4096,512]{1,0:T(8,128)(2,1)} %first_ref.1, ...), custom_call_target="tpu_custom_call" | custom-call | tf_op jit(solution)/shard_map/whole_layer/pallas_call | solution.py:770
  169.9 1.9 %copy.10 = bf16[64,4096]{1,0:T(8,128)(2,1)} copy(bf16[64,4096]{1,0:T(8,128)(2,1)} %whole_layer.1) | data formatting | bytes 1048576

commit v2 on v1

--- a/solution.py
+++ b/solution.py
@@ -17,6 +17,10 @@
 MASKED = -1e30
 MESH = pl.DeviceIdType.MESH
 VMEM_LIMIT = 60 * 1024 * 1024
+CHUNKS = 8
+AHEAD = 2
+BEHIND = 1
+HOP = 1
 
 
 def when(cond, body):
@@ -256,14 +260,15 @@
 
 def layer_kernel(
     n, rows, cap, chunks, q_ref, k_ref, v_ref, mod_ref, routes_ref, gates_ref, first_ref, second_ref,
-    out_ref, att, bias, keys, vals, line, tokens, stage, chooser, tables, stats, normed, first, second,
-    hidden, part, r1, r2, pair, acc_in, acc_out,
+    out_ref, att, asked, bias, keys, vals, line, tokens, stage, chooser, spreader, tables, stats, normed,
+    first, second, hidden, part, r1, r2, pair, acc_in, acc_out,
     own_sem, kv_send, kv_recv, table_send, table_recv, stat_send, stat_recv, out_send, line_recv,
-    token_recv, back_send, s1_recv, s2_recv, pair_recv, acc_recv,
+    token_recv, rest_send, back_send, s1_recv, s2_recv, pair_recv, acc_recv,
 ):
     planes = n // SPLIT
     width = first.shape[1]
-    wide = D // chunks
+    half = D // 2
+    wide = half // chunks
     me = lax.axis_index("tile")
     p = lax.div(me, SPLIT)
     y = lax.div(lax.rem(me, SPLIT), 2)
@@ -287,17 +292,28 @@
     half_way = TILE_COLS // 2
     crossing = {-1: column == half_way, 1: column == half_way - 1}
 
-    def cols(j):
-        return pl.ds(pl.multiple_of(j * wide, wide), wide)
+    def part_of_plane(plane):
+        return jnp.where(plane < planes // 2, half, 0)
+
+    mine_from = part_of_plane(p)
+    other_from = half - mine_from
+    partner_plane = lax.rem(p + planes // 2, planes)
+
+    def cols(j, base=0):
+        return pl.ds(pl.multiple_of(base + j * wide, wide), wide)
+
+    def halves(base):
+        return pl.ds(pl.multiple_of(base, half), half)
 
     def lines(buf, s):
         return buf.at[pl.ds(pl.multiple_of(s * rows, rows), rows), :]
 
     loads = [
-        pltpu.make_async_copy(k_ref, lines(keys, 1), own_sem.at[0]),
-        pltpu.make_async_copy(v_ref, lines(vals, 1), own_sem.at[1]),
-        pltpu.make_async_copy(first_ref, first, own_sem.at[2]),
-        pltpu.make_async_copy(second_ref, second, own_sem.at[3]),
+        pltpu.make_async_copy(q_ref.at[:, halves(mine_from)], lines(asked, 0), own_sem.at[0]),
+        pltpu.make_async_copy(k_ref.at[:, halves(mine_from)], lines(keys, 1), own_sem.at[1]),
+        pltpu.make_async_copy(v_ref.at[:, halves(mine_from)], lines(vals, 1), own_sem.at[2]),
+        pltpu.make_async_copy(first_ref, first, own_sem.at[3]),
+        pltpu.make_async_copy(second_ref, second, own_sem.at[4]),
     ]
     for load in loads:
         load.start()
@@ -314,24 +330,29 @@
     def slot_there(level, side):
         return jnp.where(crossing[side], 1 - level, level) * 3 + 1 - side
 
-    bufs = (keys, vals)
+    bufs = (keys, vals, asked)
+    given = (k_ref, v_ref, q_ref)
 
     def place(i, s, j):
         return bufs[i].at[pl.ds(pl.multiple_of(s * rows, rows), rows), cols(j)]
 
     def over_vertical(i, j):
         return remote(
-            (k_ref, v_ref)[i].at[:, cols(j)], place(i, 4, j), kv_send.at[i, j], kv_recv.at[8 + i, j], partner
+            given[i].at[:, cols(j, other_from)],
+            place(i, 4 if i < 2 else 1, j),
+            kv_send.at[i, j],
+            kv_recv.at[8 + i if i < 2 else 12, j],
+            partner,
         )
 
     def over_side(level, index, i, j):
         side = sides[index][0]
         there = slot_there(level, side)
-        source = (k_ref, v_ref)[i].at[:, cols(j)] if level == 0 else place(i, 4, j)
+        source = given[i].at[:, cols(j, mine_from)] if level == 0 else place(i, 4, j)
         return remote(
             source,
             place(i, there, j),
-            kv_send.at[2 + level * 4 + index * 2 + i, j],
+            kv_send.at[3 + level * 4 + index * 2 + i, j],
             kv_recv.at[there * 2 + i, j],
             beside_tile(side),
         )
@@ -340,8 +361,10 @@
         remote(ref, ref, own_sem.at[0], sem, me).wait_recv()
 
     def send_own(j):
-        for i in (0, 1):
+        for i in range(3):
             over_vertical(i, j).start()
+
+    def send_side(j):
         for i in (0, 1):
             for index, (_, exists) in enumerate(sides):
                 when(exists, over_side(0, index, i, j).start)
@@ -352,8 +375,9 @@
             for index, (_, exists) in enumerate(sides):
                 when(exists, over_side(1, index, i, j).start)
 
-    for j in range(min(2, chunks)):
+    for j in range(min(AHEAD, chunks)):
         send_own(j)
+        send_side(j)
 
     expert = lax.broadcasted_iota(jnp.int32, (8, rows), 0)
     named = [routes_ref[k : k + 1, :] == expert for k in (0, 1)]
@@ -380,8 +404,8 @@
         copy.start()
 
     span = 6 * rows
-    where = lax.broadcasted_iota(jnp.int32, (rows, span), 1)
-    penalty = jnp.zeros((rows, span), jnp.float32)
+    where = lax.broadcasted_iota(jnp.int32, (8, span), 1)
+    penalty = jnp.zeros((8, span), jnp.float32)
     for s in range(6):
         for side, exists in sides:
             if side != s % 3 - 1:
@@ -390,26 +414,30 @@
             penalty = jnp.where(here, jnp.where(exists, 0.0, MASKED), penalty)
 
             def clear(s=s):
-                for buf in bufs:
-                    buf[s * rows : (s + 1) * rows, :] = jnp.zeros((rows, D), buf.dtype)
+                for buf in (keys, vals):
+                    buf[s * rows : (s + 1) * rows, :] = jnp.zeros((rows, half), buf.dtype)
 
             pl.when(jnp.logical_not(exists))(clear)
     bias[...] = penalty
-    for load in loads[:2]:
+    for load in loads[:3]:
         load.wait()
-    for target in others:
-        landed(tables.at[target], table_recv.at[target])
 
     slot_line = lax.broadcasted_iota(jnp.int32, (cap, rows), 0).astype(jnp.float32)
 
     def chosen(tile_there, e):
         return tables[tile_there, pl.ds(e, 1), :] == slot_line
 
-    for plane in range(planes):
-        for place_in, e in ((0, p), (1, outer_expert)):
-            chooser[plane, place_in * cap : (place_in + 1) * cap, :] = (
-                chosen(device(plane, y, c), e).astype(jnp.float32).astype(jnp.bfloat16)
-            )
+    def choose():
+        for target in others:
+            landed(tables.at[target], table_recv.at[target])
+        chooser[...] = jnp.zeros(chooser.shape, chooser.dtype)
+        for plane in range(planes):
+            for place_in, e in ((0, p), (1, outer_expert)):
+                found = chosen(device(plane, y, c), e).astype(jnp.float32).astype(jnp.bfloat16)
+                at = place_in * 2 * cap
+                spreader[plane, place_in * cap : (place_in + 1) * cap, :] = found
+                chooser[plane, at : at + cap, :rows] = found
+                chooser[(plane + planes // 2) % planes, at + cap : at + 2 * cap, rows:] = found
 
     scale = 1.0 / math.sqrt(HEAD_DIM)
 
@@ -419,12 +447,13 @@
                 s = level * 3 + 1 + side
                 for i in (0, 1):
                     when(exists, functools.partial(landed, place(i, s, j), kv_recv.at[s * 2 + i, j]))
+        landed(place(2, 1, j), kv_recv.at[12, j])
         for extra in range(wide // HEAD_DIM):
             at = pl.ds(pl.multiple_of(j * wide + extra * HEAD_DIM, HEAD_DIM), HEAD_DIM)
             scores = lax.dot_general(
-                q_ref[:, at], keys[:, at], (((1,), (1,)), ((), ())), preferred_element_type=jnp.float32
+                asked[:, at], keys[:, at], (((1,), (1,)), ((), ())), preferred_element_type=jnp.float32
             )
-            scores = scores * scale + bias[...]
+            scores = scores * scale + bias[0:1, :]
             raised = jnp.exp(scores - jnp.max(scores, axis=-1, keepdims=True))
             probs = (raised * (1.0 / jnp.sum(raised, axis=-1, keepdims=True))).astype(jnp.bfloat16)
             att[:, at] = jnp.dot(probs, vals[:, at], preferred_element_type=jnp.float32).astype(att.dtype)
@@ -443,6 +472,13 @@
             outer_device,
         )
 
+    def rest_copy(src, j):
+        ref = line.at[src, pl.ds(rows, rows), cols(j)]
+        return remote(ref, ref, rest_send.at[j], line_recv.at[src, j], outer_device)
+
+    def rest_landed(j):
+        landed(line.at[partner_plane, pl.ds(rows, rows), cols(j)], line_recv.at[partner_plane, j])
+
     def plane_copy(k, src, j, index):
         ref = tokens.at[device(src, y, c), :, cols(j)]
         return remote(
@@ -457,10 +493,10 @@
     far = jnp.where(at_end, p + 3 * toward, p + 2 * toward)
     second_plane = jnp.where(at_end, p + 2 * toward, outer)
     sources = [
-        (p, 1, True, middle),
-        (inner, 2, False, middle),
-        (second_plane, jnp.where(at_end, 3, 2), middle, False),
-        (far, jnp.where(at_end, 4, 3), False, middle),
+        (p, BEHIND, True, middle),
+        (inner, BEHIND + HOP, False, middle),
+        (second_plane, BEHIND + HOP * jnp.where(at_end, 2, 1), middle, False),
+        (far, BEHIND + HOP * jnp.where(at_end, 3, 2), False, middle),
     ]
 
     def relay(k, j):
@@ -476,14 +512,16 @@
                 pl.when(middle)(lambda: landed(line.at[src, :, cols(jj)], line_recv.at[src, jj]))
             if whole is not False:
                 when(whole, raw_copy(k, src, jj).start)
+            if k == 1:
+                pl.when(middle)(rest_copy(src, jj).start)
 
             def pick():
                 rows_here = att[:, cols(jj)] if k == 0 else line[src, :, cols(jj)]
                 picked = jnp.dot(chooser[src], rows_here, preferred_element_type=jnp.float32).astype(
                     tokens.dtype
                 )
-                tokens[there, :, cols(jj)] = picked[:cap]
-                stage[src, :, cols(jj)] = picked[cap:]
+                tokens[there, :, cols(jj)] = picked[: 2 * cap]
+                stage[src, :, cols(jj)] = picked[2 * cap :]
 
             when(True if k == 0 else middle, pick)
             if out is not False:
@@ -495,7 +533,7 @@
 
     def pass_on(k, j):
         src, behind, _, _ = sources[k]
-        jj = j - behind - 1
+        jj = j - behind - HOP
 
         def go():
             there = device(src, 1 - y, c)
@@ -511,27 +549,34 @@
             pass_on(k, j)
 
     def stream(j, carry):
-        pl.when(j + 2 < chunks)(lambda: send_own(j + 2))
         pl.when(j < chunks)(lambda: send_vertical(j))
-        pl.when(j >= 1)(lambda: attend(j - 1))
+
+        def more():
+            send_own(j + AHEAD)
+            send_side(j + AHEAD)
+
+        pl.when(j + AHEAD < chunks)(more)
+        pl.when(j == BEHIND)(choose)
+        pl.when(j >= BEHIND)(lambda: attend(j - BEHIND))
         move(j)
         return carry
 
-    lax.fori_loop(0, chunks + 1, stream, 0)
+    lax.fori_loop(0, chunks + BEHIND, stream, 0)
 
     token = lax.broadcasted_iota(jnp.int32, (16, rows), 1)
     line_of = lax.broadcasted_iota(jnp.int32, (16, rows), 0)
-    mean_row = jnp.zeros((1, rows), jnp.float32)
-    rate_row = jnp.zeros((1, rows), jnp.float32)
-    for step in range(rows // 16):
+    row_number = lax.broadcasted_iota(jnp.int32, (8, rows), 0)
+    found = jnp.zeros((8, rows), jnp.float32)
+    for step in range(2 * rows // 16):
         some = att[step * 16 : (step + 1) * 16, :].astype(jnp.float32)
         mean = jnp.mean(some, axis=-1, keepdims=True)
         some = some - mean
-        rate = lax.rsqrt(jnp.mean(some * some, axis=-1, keepdims=True) + EPSILON)
-        same = token == line_of + step * 16
-        mean_row = mean_row + jnp.sum(jnp.where(same, mean, 0.0), axis=0, keepdims=True)
-        rate_row = rate_row + jnp.sum(jnp.where(same, rate, 0.0), axis=0, keepdims=True)
-    stats[me] = jnp.where(lax.broadcasted_iota(jnp.int32, (8, rows), 0) == 0, mean_row, rate_row)
+        spread = jnp.mean(some * some, axis=-1, keepdims=True)
+        which, at = divmod(step * 16, rows)
+        for kind, value in enumerate((mean, spread)):
+            row = jnp.sum(jnp.where(token == line_of + at, value, 0.0), axis=0, keepdims=True)
+            found = found + jnp.where(row_number == 2 * which + kind, row, 0.0)
+    stats[me] = found
     for copy in tell(stats, stat_send, stat_recv):
         copy.start()
 
@@ -539,10 +584,10 @@
         move(j)
         return carry
 
-    lax.fori_loop(chunks + 1, chunks + 5, drain, 0)
+    lax.fori_loop(chunks + BEHIND, chunks + BEHIND + 4 * HOP, drain, 0)
     for target in others:
         landed(stats.at[target], stat_recv.at[target])
-    for load in loads[2:]:
+    for load in loads[3:]:
         load.wait()
 
     order = [
@@ -551,6 +596,15 @@
         jnp.where(at_end, inner, outer),
         p,
     ]
+    def arrive(j, carry):
+        for plane in range(planes):
+            for yy in (0, 1):
+                there = device(plane, yy, 1 - c)
+                landed(tokens.at[there, :, cols(j)], token_recv.at[there, j])
+        pl.when(at_end)(lambda: rest_landed(j))
+        return carry
+
+    lax.fori_loop(0, chunks, arrive, 0)
     group = SPLIT * cap
     chunk = min(width, 256)
     chunk_out = 512
@@ -564,25 +618,24 @@
     def compute(i):
         plane = order[i]
 
-        def arrive(j, carry):
-            for yy in (0, 1):
-                there = device(plane, yy, 1 - c)
-                landed(tokens.at[there, :, cols(j)], token_recv.at[there, j])
-            return carry
-
-        lax.fori_loop(0, chunks, arrive, 0)
-
         def normalise(t, carry):
             there = plane * SPLIT + t
-            mean = picked_column(there, stats[there, 0:1, :])
-            rate = picked_column(there, stats[there, 1:2, :])
+            across = lax.rem(there + TILE_COLS, n)
+            mean_here, mean_there = stats[there, 0:1, :], stats[across, 2:3, :]
+            apart = 0.5 * (mean_here - mean_there)
+            spread = 0.5 * (stats[there, 1:2, :] + stats[across, 3:4, :]) + apart * apart
+            mean = picked_column(there, 0.5 * (mean_here + mean_there))
+            rate = picked_column(there, lax.rsqrt(spread + EPSILON))
             at = pl.ds(pl.multiple_of(t * cap, 16), cap)
-            for step in range(D // chunk_out):
-                some = slice(step * chunk_out, (step + 1) * chunk_out)
-                value = (tokens[there, :, some].astype(jnp.float32) - mean) * rate
-                normed[at, some] = (value * (1.0 + mod_ref[1:2, some]) + mod_ref[0:1, some]).astype(
-                    normed.dtype
-                )
+            base = part_of_plane(plane)
+            for source, lower, start in ((there, 0, base), (across, cap, half - base)):
+                for step in range(half // chunk_out):
+                    some = slice(step * chunk_out, (step + 1) * chunk_out)
+                    to = pl.ds(pl.multiple_of(start + step * chunk_out, chunk_out), chunk_out)
+                    value = (tokens[source, lower : lower + cap, some].astype(jnp.float32) - mean) * rate
+                    normed[at, to] = (value * (1.0 + mod_ref[1:2, to]) + mod_ref[0:1, to]).astype(
+                        normed.dtype
+                    )
             return carry
 
         lax.fori_loop(0, SPLIT, normalise, 0)
@@ -674,7 +727,7 @@
     def spread_out(plane, both, at):
         amount = 2 * cap if both else cap
         return lax.dot_general(
-            chooser[plane, :amount, :],
+            spreader[plane, :amount, :],
             pair[plane, :amount, at],
             (((0,), (0,)), ((), ())),
             preferred_element_type=jnp.float32,
@@ -695,13 +748,16 @@
                 if extra:
                     total = total + acc_in[plane, :, at].astype(jnp.float32)
                 if last:
-                    out_ref[:, at] = (att[:, at].astype(jnp.float32) + mod_ref[2:3, at] * total).astype(
+                    out_ref[:, at] = (mod_ref[2:3, at] * total + out_ref[:, at].astype(jnp.float32)).astype(
                         out_ref.dtype
                     )
                 else:
                     acc_out[plane, :, at] = total.astype(acc_out.dtype)
                 return carry
 
+            if last:
+                out_ref[:, halves(mine_from)] = att[:rows, :]
+                out_ref[:, halves(other_from)] = line[partner_plane, rows:, :]
             lax.fori_loop(0, D // chunk_out, body, 0)
             if not last:
                 rows_home(i).start()
@@ -723,8 +779,10 @@
     fold_home(planes - 1)
 
     def left(j, carry):
+        for i in range(3):
+            over_vertical(i, j).wait_send()
+        pl.when(middle)(rest_copy(inner, j).wait_send)
         for i in (0, 1):
-            over_vertical(i, j).wait_send()
             for level in (0, 1):
                 for index, (_, exists) in enumerate(sides):
                     when(exists, over_side(level, index, i, j).wait_send)
@@ -762,7 +820,7 @@
     width = expert_in.shape[1]
     planes = n // SPLIT
     cap = 3 * rows // planes
-    chunks = 8
+    chunks = CHUNKS
     vmem = pl.BlockSpec(memory_space=pltpu.VMEM)
     hbm = pl.BlockSpec(memory_space=pl.ANY)
     dma = pltpu.SemaphoreType.DMA
@@ -771,16 +829,18 @@
         functools.partial(layer_kernel, n, rows, cap, chunks),
         name="whole_layer",
         out_shape=jax.ShapeDtypeStruct((rows, D), bf),
-        in_specs=[vmem, hbm, hbm, vmem, vmem, vmem, hbm, hbm],
+        in_specs=[hbm, hbm, hbm, vmem, vmem, vmem, hbm, hbm],
         out_specs=vmem,
         scratch_shapes=[
-            pltpu.VMEM((rows, D), bf),
-            pltpu.VMEM((rows, 6 * rows), jnp.float32),
-            pltpu.VMEM((6 * rows, D), bf),
-            pltpu.VMEM((6 * rows, D), bf),
-            pltpu.VMEM((planes, rows, D), bf),
-            pltpu.VMEM((n, cap, D), bf),
-            pltpu.VMEM((planes, cap, D), bf),
+            pltpu.VMEM((2 * rows, D // 2), bf),
+            pltpu.VMEM((2 * rows, D // 2), bf),
+            pltpu.VMEM((8, 6 * rows), jnp.float32),
+            pltpu.VMEM((6 * rows, D // 2), bf),
+            pltpu.VMEM((6 * rows, D // 2), bf),
+            pltpu.VMEM((planes, 2 * rows, D // 2), bf),
+            pltpu.VMEM((n, 2 * cap, D // 2), bf),
+            pltpu.VMEM((planes, 2 * cap, D // 2), bf),
+            pltpu.VMEM((planes, 4 * cap, 2 * rows), bf),
             pltpu.VMEM((planes, 2 * cap, rows), bf),
             pltpu.VMEM((n, 16, rows), jnp.float32),
             pltpu.VMEM((n, 8, rows), jnp.float32),
@@ -794,9 +854,9 @@
             pltpu.VMEM((planes, 2 * cap, D), bf),
             pltpu.VMEM((planes, rows, D), bf),
             pltpu.VMEM((planes, rows, D), bf),
-            dma((4,)),
-            dma((10, chunks)),
-            dma((12, chunks)),
+            dma((5,)),
+            dma((11, chunks)),
+            dma((13, chunks)),
             dma((n - 1,)),
             dma((n,)),
             dma((n - 1,)),
@@ -804,6 +864,7 @@
             dma((planes, 5, chunks)),
             dma((planes, chunks)),
             dma((n, chunks)),
+            dma((chunks,)),
             dma((planes, 4)),
             dma((planes, 2)),
             dma((planes,)),

time: 172 us -> 150 us (0.87)
  Pallas kernels: 170 us -> 148 us
    pallas_call x1, Pallas kernels: 170 us -> 148 us  [layer(): pl.pallas_call(functools.partial(layer_kernel, n, rows, cap, chunks), nam...]
where the time goes in v2:
time: 150 us
  Pallas kernels  148 us (99%)
  local copies, waits for them, and re-layouts  1.87 us (1%)
    pallas_call x1, Pallas kernels, layer(): pl.pallas_call(functools.partial(layer_kernel, n, rows, cap, chunks), nam...  148 us

profile of v2, /device:TPU:0, one launch (start us, length us, event | category | flops | bytes accessed | tf_op | source)
XLA Modules:
  0.0 150.2 jit_solution(11710085190589216463)
XLA Ops:
  0.0 148.3 %whole_layer.1 = bf16[64,4096]{1,0:T(8,128)(2,1)} custom-call(bf16[64,4096]{1,0:T(8,128)(2,1)} %q_ref.1, bf16[64,4096]{1,0:T(8,128)(2,1)} %k_ref.1, bf16[64,4096]{1,0:T(8,128)(2,1)} %v_ref.1, f32[3,4096]{1,0:T(4,128)} %mod_ref.1, s32[2,64]{1,0:T(2,128)} %bitcast.2, s32[2,64]{1,0:T(2,128)} %bitcast.3, bf16[4096,512]{1,0:T(8,128)(2,1)} %first_ref.1, ...), custom_call_target="tpu_custom_call" | custom-call | tf_op jit(solution)/shard_map/whole_layer/pallas_call | solution.py:828
  148.3 1.9 %copy.10 = bf16[64,4096]{1,0:T(8,128)(2,1)} copy(bf16[64,4096]{1,0:T(8,128)(2,1)} %whole_layer.1) | data formatting | bytes 1048576

commit v3 on v2

--- a/solution.py
+++ b/solution.py
@@ -19,8 +19,10 @@
 VMEM_LIMIT = 60 * 1024 * 1024
 CHUNKS = 8
 AHEAD = 2
-BEHIND = 1
-HOP = 1
+BEHIND = 2
+HOP = 2
+BACK_CHUNKS = 4
+BACK_LAGS = (1, 4, 6)
 
 
 def when(cond, body):
@@ -259,7 +261,7 @@
 
 
 def layer_kernel(
-    n, rows, cap, chunks, q_ref, k_ref, v_ref, mod_ref, routes_ref, gates_ref, first_ref, second_ref,
+    n, rows, cap, chunks, backs, q_ref, k_ref, v_ref, mod_ref, routes_ref, gates_ref, first_ref, second_ref,
     out_ref, att, asked, bias, keys, vals, line, tokens, stage, chooser, spreader, tables, stats, normed,
     first, second, hidden, part, r1, r2, pair, acc_in, acc_out,
     own_sem, kv_send, kv_recv, table_send, table_recv, stat_send, stat_recv, out_send, line_recv,
@@ -606,20 +608,25 @@
 
     lax.fori_loop(0, chunks, arrive, 0)
     group = SPLIT * cap
-    chunk = min(width, 256)
-    chunk_out = 512
-
-    def block(buf, index):
-        return buf.at[pl.ds(pl.multiple_of(index * cap, 16), cap), :]
+    chunk = 512
+    span_back = D // backs
+
+    def home_of(i):
+        return jnp.where(i == 0, order[0], jnp.where(i == 1, order[1], jnp.where(i == 2, order[2], order[3])))
+
+    def block(buf, index, count, j):
+        return buf.at[pl.ds(pl.multiple_of(index * cap, 16), count * cap), back_cols(j)]
+
+    def back_cols(j):
+        return pl.ds(pl.multiple_of(j * span_back, span_back), span_back)
 
     def picked_column(tile_there, row):
         return jnp.sum(jnp.where(chosen(tile_there, p), row, 0.0), axis=1, keepdims=True)
 
-    def compute(i):
-        plane = order[i]
-
+    def start_group(plane):
         def normalise(t, carry):
-            there = plane * SPLIT + t
+            yy, cc = lax.rem(t, 2), lax.div(t, 2)
+            there = device(plane, yy, cc)
             across = lax.rem(there + TILE_COLS, n)
             mean_here, mean_there = stats[there, 0:1, :], stats[across, 2:3, :]
             apart = 0.5 * (mean_here - mean_there)
@@ -629,9 +636,9 @@
             at = pl.ds(pl.multiple_of(t * cap, 16), cap)
             base = part_of_plane(plane)
             for source, lower, start in ((there, 0, base), (across, cap, half - base)):
-                for step in range(half // chunk_out):
-                    some = slice(step * chunk_out, (step + 1) * chunk_out)
-                    to = pl.ds(pl.multiple_of(start + step * chunk_out, chunk_out), chunk_out)
+                for step in range(half // chunk):
+                    some = slice(step * chunk, (step + 1) * chunk)
+                    to = pl.ds(pl.multiple_of(start + step * chunk, chunk), chunk)
                     value = (tokens[source, lower : lower + cap, some].astype(jnp.float32) - mean) * rate
                     normed[at, to] = (value * (1.0 + mod_ref[1:2, to]) + mod_ref[0:1, to]).astype(
                         normed.dtype
@@ -639,90 +646,74 @@
             return carry
 
         lax.fori_loop(0, SPLIT, normalise, 0)
-
-        def one(step, carry):
-            at = pl.ds(pl.multiple_of(step * chunk, chunk), chunk)
-            raw = jnp.dot(normed[...], first[:, at], preferred_element_type=jnp.float32)
-            hidden[:, at] = jax.nn.gelu(raw, approximate=True).astype(hidden.dtype)
-            return carry
-
-        lax.fori_loop(0, width // chunk, one, 0)
-        mine = pl.ds(pl.multiple_of(plane * group, 16), group)
-
-        def two(step, carry):
-            at = pl.ds(pl.multiple_of(step * chunk_out, chunk_out), chunk_out)
-            raw = jnp.dot(hidden[...], second[:, at], preferred_element_type=jnp.float32)
-            part[mine, at] = raw.astype(part.dtype)
-            return carry
-
-        lax.fori_loop(0, D // chunk_out, two, 0)
-        for yy in (0, 1):
-            to_twin(i, yy).start()
-
-    def to_twin(i, yy):
-        plane = order[i]
+        raw = jnp.dot(normed[...], first[...], preferred_element_type=jnp.float32)
+        hidden[...] = jax.nn.gelu(raw, approximate=True).astype(hidden.dtype)
+
+    def to_twin(plane, j):
         return remote(
-            block(part, device(plane, yy, 1 - c)),
-            block(r1, plane * 2 + yy),
-            back_send.at[i, yy],
-            s1_recv.at[plane, yy],
+            block(part, plane * SPLIT + (1 - c) * 2, 2, j),
+            block(r1, plane * 2, 2, j),
+            back_send.at[plane, 0, j],
+            s1_recv.at[plane, j],
             twin,
         )
 
-    def to_beside(i):
-        plane = order[i]
+    def to_beside(plane, j):
         return remote(
-            block(part, device(plane, 1 - y, c)), block(r2, plane), back_send.at[i, 2], s2_recv.at[plane], beside
+            block(part, plane * SPLIT + c * 2 + 1 - y, 1, j),
+            block(r2, plane, 1, j),
+            back_send.at[plane, 1, j],
+            s2_recv.at[plane, j],
+            beside,
         )
 
-    def fold_twin(i):
-        plane = order[i]
-        for yy in (1 - y, y):
-            landed(block(r1, plane * 2 + yy), s1_recv.at[plane, yy])
-            base = device(plane, yy, c) * cap
-            from_there = (plane * 2 + yy) * cap
-
-            def body(step, carry):
-                at = pl.ds(pl.multiple_of(base + step * 16, 16), 16)
-                extra = r1[pl.ds(pl.multiple_of(from_there + step * 16, 16), 16), :]
-                part[at, :] = (part[at, :].astype(jnp.float32) + extra.astype(jnp.float32)).astype(part.dtype)
-                return carry
-
-            lax.fori_loop(0, cap // 16, body, 0)
-            if yy is not y:
-                to_beside(i).start()
-
-    def fold_beside(i):
-        plane = order[i]
-        there = device(plane, y, c)
-        landed(block(r2, plane), s2_recv.at[plane])
-        weight = picked_column(there, tables[there, pl.ds(8 + p, 1), :])
-        ours = pl.ds(pl.multiple_of(there * cap, 16), cap)
-        theirs = pl.ds(pl.multiple_of(plane * cap, 16), cap)
-        for step in range(D // chunk_out):
-            some = slice(step * chunk_out, (step + 1) * chunk_out)
-            total = part[ours, some].astype(jnp.float32) + r2[theirs, some].astype(jnp.float32)
-            pair[plane, :cap, some] = (total * weight).astype(pair.dtype)
-
-    def slots_home(i):
-        plane = order[i]
+    def slots_home(plane, j):
         return remote(
-            pair.at[plane, pl.ds(0, cap), :],
-            pair.at[plane, pl.ds(cap, cap), :],
-            back_send.at[i, 3],
-            pair_recv.at[plane],
+            pair.at[plane, pl.ds(0, cap), back_cols(j)],
+            pair.at[plane, pl.ds(cap, cap), back_cols(j)],
+            back_send.at[plane, 2, j],
+            pair_recv.at[plane, j],
             inner_device,
         )
 
-    def rows_home(i):
-        plane = order[i]
+    def rows_home(plane, j):
         return remote(
-            acc_out.at[plane],
-            acc_in.at[plane],
-            back_send.at[i, 3],
-            acc_recv.at[plane],
-            outer_device if i == 2 else inner_device,
+            acc_out.at[plane, :, back_cols(j)],
+            acc_in.at[plane, :, back_cols(j)],
+            back_send.at[plane, 3, j],
+            acc_recv.at[plane, j],
+            device(jnp.where(plane == outer, outer, inner), y, c),
         )
+
+    def produce(i, j):
+        plane = home_of(i)
+        pl.when(j == 0)(lambda: start_group(plane))
+        raw = jnp.dot(hidden[...], second[:, back_cols(j)], preferred_element_type=jnp.float32)
+        mine = pl.ds(pl.multiple_of(plane * group, 16), group)
+        part[mine, back_cols(j)] = raw.astype(part.dtype)
+        to_twin(plane, j).start()
+
+    def fold_twin(i, j):
+        plane = home_of(i)
+        landed(block(r1, plane * 2, 2, j), s1_recv.at[plane, j])
+        for yy in (1 - y, y):
+            at = pl.ds(pl.multiple_of((plane * SPLIT + c * 2 + yy) * cap, 16), cap)
+            there = pl.ds(pl.multiple_of((plane * 2 + yy) * cap, 16), cap)
+            total = part[at, back_cols(j)].astype(jnp.float32) + r1[there, back_cols(j)].astype(jnp.float32)
+            part[at, back_cols(j)] = total.astype(part.dtype)
+            if yy is not y:
+                to_beside(plane, j).start()
+
+    def fold_beside(i, j):
+        plane = home_of(i)
+        there = device(plane, y, c)
+        landed(block(r2, plane, 1, j), s2_recv.at[plane, j])
+        weight = picked_column(there, tables[there, pl.ds(8 + p, 1), :])
+        ours = pl.ds(pl.multiple_of((plane * SPLIT + c * 2 + y) * cap, 16), cap)
+        theirs = pl.ds(pl.multiple_of(plane * cap, 16), cap)
+        total = part[ours, back_cols(j)].astype(jnp.float32) + r2[theirs, back_cols(j)].astype(jnp.float32)
+        pair[plane, :cap, back_cols(j)] = (total * weight).astype(pair.dtype)
+        pl.when(jnp.logical_and(at_end, plane != p))(slots_home(plane, j).start)
 
     def spread_out(plane, both, at):
         amount = 2 * cap if both else cap
@@ -733,50 +724,43 @@
             preferred_element_type=jnp.float32,
         )
 
-    def fold_home(i):
-        plane = order[i]
+    def fold_home(i, j):
+        plane = home_of(i)
+        at = back_cols(j)
 
         def fold(both, extra, last):
             if both:
-                landed(pair.at[plane, pl.ds(cap, cap), :], pair_recv.at[plane])
+                landed(pair.at[plane, pl.ds(cap, cap), at], pair_recv.at[plane, j])
             if extra:
-                landed(acc_in.at[plane], acc_recv.at[plane])
-
-            def body(step, carry):
-                at = pl.ds(pl.multiple_of(step * chunk_out, chunk_out), chunk_out)
-                total = spread_out(plane, both, at)
-                if extra:
-                    total = total + acc_in[plane, :, at].astype(jnp.float32)
-                if last:
-                    out_ref[:, at] = (mod_ref[2:3, at] * total + out_ref[:, at].astype(jnp.float32)).astype(
-                        out_ref.dtype
-                    )
-                else:
-                    acc_out[plane, :, at] = total.astype(acc_out.dtype)
-                return carry
-
+                landed(acc_in.at[plane, :, at], acc_recv.at[plane, j])
+            total = spread_out(plane, both, at)
+            if extra:
+                total = total + acc_in[plane, :, at].astype(jnp.float32)
             if last:
-                out_ref[:, halves(mine_from)] = att[:rows, :]
-                out_ref[:, halves(other_from)] = line[partner_plane, rows:, :]
-            lax.fori_loop(0, D // chunk_out, body, 0)
-            if not last:
-                rows_home(i).start()
-
-        if i == 3:
-            pl.when(at_end)(lambda: fold(False, True, True))
-            pl.when(middle)(lambda: fold(True, True, True))
-        else:
-            pl.when(at_end)(slots_home(i).start)
-            pl.when(middle)(lambda: fold(i < 2, i == 2, False))
-
-    for i in range(planes):
-        compute(i)
-        fold_twin(i)
-        if i > 0:
-            fold_beside(i - 1)
-            fold_home(i - 1)
-    fold_beside(planes - 1)
-    fold_home(planes - 1)
+                out_ref[:, at] = (mod_ref[2:3, at] * total + out_ref[:, at].astype(jnp.float32)).astype(
+                    out_ref.dtype
+                )
+            else:
+                acc_out[plane, :, at] = total.astype(acc_out.dtype)
+                rows_home(plane, j).start()
+
+        pl.when(jnp.logical_and(at_end, i == 3))(lambda: fold(False, True, True))
+        pl.when(jnp.logical_and(middle, i == 3))(lambda: fold(True, True, True))
+        pl.when(jnp.logical_and(middle, i == 2))(lambda: fold(False, True, False))
+        pl.when(jnp.logical_and(middle, i < 2))(lambda: fold(True, False, False))
+
+    out_ref[:, halves(mine_from)] = att[:rows, :]
+    out_ref[:, halves(other_from)] = line[partner_plane, rows:, :]
+    units = planes * backs
+
+    def give_back(u, carry):
+        for behind, act in ((0, produce), (BACK_LAGS[0], fold_twin), (BACK_LAGS[1], fold_beside), (BACK_LAGS[2], fold_home)):
+            at = u - behind
+            i, j = lax.div(at, backs), lax.rem(at, backs)
+            pl.when(jnp.logical_and(at >= 0, at < units))(functools.partial(act, i, j))
+        return carry
+
+    lax.fori_loop(0, units + BACK_LAGS[2], give_back, 0)
 
     def left(j, carry):
         for i in range(3):
@@ -799,13 +783,17 @@
     lax.fori_loop(0, chunks, left, 0)
     for copy in tell(tables, table_send, table_recv) + tell(stats, stat_send, stat_recv):
         copy.wait_send()
-    for i in range(planes):
-        for yy in (0, 1):
-            to_twin(i, yy).wait_send()
-        to_beside(i).wait_send()
-        if i < planes - 1:
-            pl.when(at_end)(slots_home(i).wait_send)
-            pl.when(middle)(rows_home(i).wait_send)
+
+    def returned(j, carry):
+        for plane in range(planes):
+            to_twin(plane, j).wait_send()
+            to_beside(plane, j).wait_send()
+            away = p != plane
+            pl.when(jnp.logical_and(at_end, away))(slots_home(plane, j).wait_send)
+            pl.when(jnp.logical_and(middle, away))(rows_home(plane, j).wait_send)
+        return carry
+
+    lax.fori_loop(0, backs, returned, 0)
 
 
 def kernel_bytes(n, rows, cap, width):
@@ -820,13 +808,13 @@
     width = expert_in.shape[1]
     planes = n // SPLIT
     cap = 3 * rows // planes
-    chunks = CHUNKS
+    chunks, backs = CHUNKS, BACK_CHUNKS
     vmem = pl.BlockSpec(memory_space=pltpu.VMEM)
     hbm = pl.BlockSpec(memory_space=pl.ANY)
     dma = pltpu.SemaphoreType.DMA
     bf = jnp.bfloat16
     return pl.pallas_call(
-        functools.partial(layer_kernel, n, rows, cap, chunks),
+        functools.partial(layer_kernel, n, rows, cap, CHUNKS, BACK_CHUNKS),
         name="whole_layer",
         out_shape=jax.ShapeDtypeStruct((rows, D), bf),
         in_specs=[hbm, hbm, hbm, vmem, vmem, vmem, hbm, hbm],
@@ -865,11 +853,11 @@
             dma((planes, chunks)),
             dma((n, chunks)),
             dma((chunks,)),
-            dma((planes, 4)),
-            dma((planes, 2)),
-            dma((planes,)),
-            dma((planes,)),
-            dma((planes,)),
+            dma((planes, 4, backs)),
+            dma((planes, backs)),
+            dma((planes, backs)),
+            dma((planes, backs)),
+            dma((planes, backs)),
         ],
         compiler_params=pltpu.CompilerParams(
             collective_id=1, has_side_effects=True, vmem_limit_bytes=VMEM_LIMIT

time: 150 us -> 131 us (0.87)
  Pallas kernels: 148 us -> 129 us
    pallas_call x1, Pallas kernels: 148 us -> 129 us  [layer(): pl.pallas_call(functools.partial(layer_kernel, n, rows, cap, CHUNKS, BACK...]
where the time goes in v3:
time: 131 us
  Pallas kernels  129 us (98%)
  local copies, waits for them, and re-layouts  1.87 us (1%)
    pallas_call x1, Pallas kernels, layer(): pl.pallas_call(functools.partial(layer_kernel, n, rows, cap, CHUNKS, BACK...  129 us

profile of v3, /device:TPU:0, one launch (start us, length us, event | category | flops | bytes accessed | tf_op | source)
XLA Modules:
  0.0 130.8 jit_solution(1299425852247626910)
XLA Ops:
  0.0 128.9 %whole_layer.1 = bf16[64,4096]{1,0:T(8,128)(2,1)} custom-call(bf16[64,4096]{1,0:T(8,128)(2,1)} %q_ref.1, bf16[64,4096]{1,0:T(8,128)(2,1)} %k_ref.1, bf16[64,4096]{1,0:T(8,128)(2,1)} %v_ref.1, f32[3,4096]{1,0:T(4,128)} %mod_ref.1, s32[2,64]{1,0:T(2,128)} %bitcast.2, s32[2,64]{1,0:T(2,128)} %bitcast.3, bf16[4096,512]{1,0:T(8,128)(2,1)} %first_ref.1, ...), custom_call_target="tpu_custom_call" | custom-call | tf_op jit(solution)/shard_map/whole_layer/pallas_call | solution.py:816
  128.9 1.9 %copy.10 = bf16[64,4096]{1,0:T(8,128)(2,1)} copy(bf16[64,4096]{1,0:T(8,128)(2,1)} %whole_layer.1) | data formatting | bytes 1048576

commit v4 on v3

--- a/solution.py
+++ b/solution.py
@@ -19,6 +19,7 @@
 VMEM_LIMIT = 60 * 1024 * 1024
 CHUNKS = 8
 AHEAD = 2
+ASIDE = 2
 BEHIND = 2
 HOP = 2
 BACK_CHUNKS = 4
@@ -317,14 +318,11 @@
         pltpu.make_async_copy(first_ref, first, own_sem.at[3]),
         pltpu.make_async_copy(second_ref, second, own_sem.at[4]),
     ]
-    for load in loads:
-        load.start()
 
     barrier = pltpu.get_barrier_semaphore()
     others = [lax.rem(me + step, n) for step in range(1, n)]
     for target in others:
         pl.semaphore_signal(barrier, inc=1, device_id={"tile": target}, device_id_type=MESH)
-    pl.semaphore_wait(barrier, n - 1)
 
     def beside_tile(side):
         return lax.rem(me + side + jnp.where(crossing[side], TILE_COLS, 0) + n, n)
@@ -376,10 +374,6 @@
             landed(place(i, 4, j), kv_recv.at[8 + i, j])
             for index, (_, exists) in enumerate(sides):
                 when(exists, over_side(1, index, i, j).start)
-
-    for j in range(min(AHEAD, chunks)):
-        send_own(j)
-        send_side(j)
 
     expert = lax.broadcasted_iota(jnp.int32, (8, rows), 0)
     named = [routes_ref[k : k + 1, :] == expert for k in (0, 1)]
@@ -394,16 +388,8 @@
         jnp.where(named[k], gates_ref[k : k + 1, :].astype(jnp.float32), 0.0) for k in (0, 1)
     )
     tables[me, 0:8, :] = jnp.where(member, count - 1.0, -1.0)
+    stats[me, 8:16, :] = jnp.where(member, count - 1.0, -1.0)
     tables[me, 8:16, :] = gate / 1024.0
-
-    def tell(ref, send, recv):
-        return [
-            remote(ref.at[me], ref.at[me], send.at[step], recv.at[me], target)
-            for step, target in enumerate(others)
-        ]
-
-    for copy in tell(tables, table_send, table_recv):
-        copy.start()
 
     span = 6 * rows
     where = lax.broadcasted_iota(jnp.int32, (8, span), 1)
@@ -421,17 +407,47 @@
 
             pl.when(jnp.logical_not(exists))(clear)
     bias[...] = penalty
+
+    column_planes = [lax.rem(p + step, planes) for step in range(1, planes)]
+
+    def tell_column(step):
+        there = device(column_planes[step], y, c)
+        return remote(tables.at[me], tables.at[me], table_send.at[step], table_recv.at[p], there)
+
+    def tell_all():
+        return [
+            remote(stats.at[me], stats.at[me], stat_send.at[step], stat_recv.at[me], target)
+            for step, target in enumerate(others)
+        ]
+
+    pl.semaphore_wait(barrier, n - 1)
+    send_own(0)
+    for step in range(planes - 1):
+        tell_column(step).start()
+    send_side(0)
+    for load in loads[:3]:
+        load.start()
+    for j in range(1, max(AHEAD, ASIDE)):
+        if j < min(AHEAD, chunks):
+            send_own(j)
+        if j < min(ASIDE, chunks):
+            send_side(j)
     for load in loads[:3]:
         load.wait()
+    for load in loads[3:]:
+        load.start()
 
     slot_line = lax.broadcasted_iota(jnp.int32, (cap, rows), 0).astype(jnp.float32)
 
     def chosen(tile_there, e):
         return tables[tile_there, pl.ds(e, 1), :] == slot_line
 
+    def picked_column(which, row):
+        return jnp.sum(jnp.where(which, row, 0.0), axis=1, keepdims=True)
+
     def choose():
-        for target in others:
-            landed(tables.at[target], table_recv.at[target])
+        for plane in column_planes:
+            landed(tables.at[device(plane, y, c)], table_recv.at[plane])
         chooser[...] = jnp.zeros(chooser.shape, chooser.dtype)
         for plane in range(planes):
             for place_in, e in ((0, p), (1, outer_expert)):
@@ -553,11 +569,8 @@
     def stream(j, carry):
         pl.when(j < chunks)(lambda: send_vertical(j))
 
-        def more():
-            send_own(j + AHEAD)
-            send_side(j + AHEAD)
-
-        pl.when(j + AHEAD < chunks)(more)
+        pl.when(j + AHEAD < chunks)(lambda: send_own(j + AHEAD))
+        pl.when(j + ASIDE < chunks)(lambda: send_side(j + ASIDE))
         pl.when(j == BEHIND)(choose)
         pl.when(j >= BEHIND)(lambda: attend(j - BEHIND))
         move(j)
@@ -578,8 +591,8 @@
         for kind, value in enumerate((mean, spread)):
             row = jnp.sum(jnp.where(token == line_of + at, value, 0.0), axis=0, keepdims=True)
             found = found + jnp.where(row_number == 2 * which + kind, row, 0.0)
-    stats[me] = found
-    for copy in tell(stats, stat_send, stat_recv):
+    stats[me, 0:8, :] = found
+    for copy in tell_all():
         copy.start()
 
     def drain(j, carry):
@@ -620,9 +633,6 @@
     def back_cols(j):
         return pl.ds(pl.multiple_of(j * span_back, span_back), span_back)
 
-    def picked_column(tile_there, row):
-        return jnp.sum(jnp.where(chosen(tile_there, p), row, 0.0), axis=1, keepdims=True)
-
     def start_group(plane):
         def normalise(t, carry):
             yy, cc = lax.rem(t, 2), lax.div(t, 2)
@@ -631,8 +641,9 @@
             mean_here, mean_there = stats[there, 0:1, :], stats[across, 2:3, :]
             apart = 0.5 * (mean_here - mean_there)
             spread = 0.5 * (stats[there, 1:2, :] + stats[across, 3:4, :]) + apart * apart
-            mean = picked_column(there, 0.5 * (mean_here + mean_there))
-            rate = picked_column(there, lax.rsqrt(spread + EPSILON))
+            which = stats[there, pl.ds(8 + p, 1), :] == slot_line
+            mean = picked_column(which, 0.5 * (mean_here + mean_there))
+            rate = picked_column(which, lax.rsqrt(spread + EPSILON))
             at = pl.ds(pl.multiple_of(t * cap, 16), cap)
             base = part_of_plane(plane)
             for source, lower, start in ((there, 0, base), (across, cap, half - base)):
@@ -708,7 +719,7 @@
         plane = home_of(i)
         there = device(plane, y, c)
         landed(block(r2, plane, 1, j), s2_recv.at[plane, j])
-        weight = picked_column(there, tables[there, pl.ds(8 + p, 1), :])
+        weight = picked_column(chosen(there, p), tables[there, pl.ds(8 + p, 1), :])
         ours = pl.ds(pl.multiple_of((plane * SPLIT + c * 2 + y) * cap, 16), cap)
         theirs = pl.ds(pl.multiple_of(plane * cap, 16), cap)
         total = part[ours, back_cols(j)].astype(jnp.float32) + r2[theirs, back_cols(j)].astype(jnp.float32)
@@ -781,7 +792,7 @@
         return carry
 
     lax.fori_loop(0, chunks, left, 0)
-    for copy in tell(tables, table_send, table_recv) + tell(stats, stat_send, stat_recv):
+    for copy in [tell_column(step) for step in range(planes - 1)] + tell_all():
         copy.wait_send()
 
     def returned(j, carry):
@@ -816,7 +827,7 @@
     return pl.pallas_call(
         functools.partial(layer_kernel, n, rows, cap, CHUNKS, BACK_CHUNKS),
         name="whole_layer",
-        out_shape=jax.ShapeDtypeStruct((rows, D), bf),
+        out_shape=pltpu.VMEM((rows, D), bf),
         in_specs=[hbm, hbm, hbm, vmem, vmem, vmem, hbm, hbm],
         out_specs=vmem,
         scratch_shapes=[
@@ -831,7 +842,7 @@
             pltpu.VMEM((planes, 4 * cap, 2 * rows), bf),
             pltpu.VMEM((planes, 2 * cap, rows), bf),
             pltpu.VMEM((n, 16, rows), jnp.float32),
-            pltpu.VMEM((n, 8, rows), jnp.float32),
+            pltpu.VMEM((n, 16, rows), jnp.float32),
             pltpu.VMEM((SPLIT * cap, D), bf),
             pltpu.VMEM((D, width), bf),
             pltpu.VMEM((width, D), bf),
@@ -845,8 +856,8 @@
             dma((5,)),
             dma((11, chunks)),
             dma((13, chunks)),
-            dma((n - 1,)),
-            dma((n,)),
+            dma((planes - 1,)),
+            dma((planes,)),
             dma((n - 1,)),
             dma((n,)),
             dma((planes, 5, chunks)),

time: 131 us -> 128 us (0.977)
  Pallas kernels: 129 us -> 127 us
    pallas_call x1, Pallas kernels: 129 us -> 127 us  [layer(): pl.pallas_call(functools.partial(layer_kernel, n, rows, cap, CHUNKS, BACK...]
where the time goes in v4:
time: 128 us; the launch traced here: 127 us
  Pallas kernels  127 us (99%)
    pallas_call x1, Pallas kernels, layer(): pl.pallas_call(functools.partial(layer_kernel, n, rows, cap, CHUNKS, BACK...  127 us

profile of v4, /device:TPU:0, one launch (start us, length us, event | category | flops | bytes accessed | tf_op | source)
XLA Modules:
  0.0 127.4 jit_solution(15377127344258843890)
XLA Ops:
  0.0 126.6 %whole_layer.1 = bf16[64,4096]{1,0:T(8,128)(2,1)S(1)} custom-call(bf16[64,4096]{1,0:T(8,128)(2,1)} %q_ref.1, bf16[64,4096]{1,0:T(8,128)(2,1)} %k_ref.1, bf16[64,4096]{1,0:T(8,128)(2,1)} %v_ref.1, f32[3,4096]{1,0:T(4,128)} %mod_ref.1, s32[2,64]{1,0:T(2,128)} %bitcast.2, s32[2,64]{1,0:T(2,128)} %bitcast.3, bf16[4096,512]{1,0:T(8,128)(2,1)} %first_ref.1, ...), custom_call_target="tpu_custom_call" | custom-call | tf_op jit(solution)/shard_map/whole_layer/pallas_call | solution.py:827
  126.6 0.8 copy.10

commit v5 on v4

--- a/solution.py
+++ b/solution.py
@@ -265,8 +265,8 @@
     n, rows, cap, chunks, backs, q_ref, k_ref, v_ref, mod_ref, routes_ref, gates_ref, first_ref, second_ref,
     out_ref, att, asked, bias, keys, vals, line, tokens, stage, chooser, spreader, tables, stats, normed,
     first, second, hidden, part, r1, r2, pair, acc_in, acc_out,
-    own_sem, kv_send, kv_recv, table_send, table_recv, stat_send, stat_recv, out_send, line_recv,
-    token_recv, rest_send, back_send, s1_recv, s2_recv, pair_recv, acc_recv,
+    own_sem, kv_send, kv_recv, table_send, table_recv, out_send, line_recv, beside_recv, twin_recv,
+    rest_sem, back_send, s1_recv, s2_recv, pair_recv, acc_recv,
 ):
     planes = n // SPLIT
     width = first.shape[1]
@@ -340,8 +340,8 @@
         return remote(
             given[i].at[:, cols(j, other_from)],
             place(i, 4 if i < 2 else 1, j),
-            kv_send.at[i, j],
-            kv_recv.at[8 + i if i < 2 else 12, j],
+            kv_send.at[0],
+            kv_recv.at[4, j],
             partner,
         )
 
@@ -352,8 +352,8 @@
         return remote(
             source,
             place(i, there, j),
-            kv_send.at[3 + level * 4 + index * 2 + i, j],
-            kv_recv.at[there * 2 + i, j],
+            kv_send.at[1 + level * 2 + index],
+            kv_recv.at[there, j],
             beside_tile(side),
         )
 
@@ -369,9 +369,12 @@
             for index, (_, exists) in enumerate(sides):
                 when(exists, over_side(0, index, i, j).start)
 
+    def bytes_of(count, at):
+        return keys.at[pl.ds(0, count * rows), at]
+
     def send_vertical(j):
+        landed(bytes_of(3, cols(j)), kv_recv.at[4, j])
         for i in (0, 1):
-            landed(place(i, 4, j), kv_recv.at[8 + i, j])
             for index, (_, exists) in enumerate(sides):
                 when(exists, over_side(1, index, i, j).start)
 
@@ -412,12 +415,12 @@
 
     def tell_column(step):
         there = device(column_planes[step], y, c)
-        return remote(tables.at[me], tables.at[me], table_send.at[step], table_recv.at[p], there)
+        return remote(tables.at[me], tables.at[me], table_send.at[0], table_recv.at[0], there)
 
     def tell_all():
         return [
-            remote(stats.at[me], stats.at[me], stat_send.at[step], stat_recv.at[me], target)
-            for step, target in enumerate(others)
+            remote(stats.at[me], stats.at[me], table_send.at[1], table_recv.at[1], target)
+            for target in others
         ]
 
     pl.semaphore_wait(barrier, n - 1)
@@ -446,8 +449,7 @@
         return jnp.sum(jnp.where(which, row, 0.0), axis=1, keepdims=True)
 
     def choose():
-        for plane in column_planes:
-            landed(tables.at[device(plane, y, c)], table_recv.at[plane])
+        landed(tables.at[pl.ds(0, planes - 1)], table_recv.at[0])
         chooser[...] = jnp.zeros(chooser.shape, chooser.dtype)
         for plane in range(planes):
             for place_in, e in ((0, p), (1, outer_expert)):
@@ -463,9 +465,7 @@
         for level in (0, 1):
             for side, exists in sides:
                 s = level * 3 + 1 + side
-                for i in (0, 1):
-                    when(exists, functools.partial(landed, place(i, s, j), kv_recv.at[s * 2 + i, j]))
-        landed(place(2, 1, j), kv_recv.at[12, j])
+                when(exists, functools.partial(landed, bytes_of(2, cols(j)), kv_recv.at[s, j]))
         for extra in range(wide // HEAD_DIM):
             at = pl.ds(pl.multiple_of(j * wide + extra * HEAD_DIM, HEAD_DIM), HEAD_DIM)
             scores = lax.dot_general(
@@ -478,35 +478,31 @@
 
     def raw_copy(k, src, j):
         source = att.at[:, cols(j)] if k == 0 else line.at[src, :, cols(j)]
-        return remote(source, line.at[src, :, cols(j)], out_send.at[k, 0, j], line_recv.at[src, j], inner_device)
+        return remote(source, line.at[src, :, cols(j)], out_send.at[k, 0], line_recv.at[src, j], inner_device)
 
     def outer_copy(k, src, j):
         there = device(src, y, c)
         return remote(
             stage.at[src, :, cols(j)],
             tokens.at[there, :, cols(j)],
-            out_send.at[k, 1, j],
-            token_recv.at[there, j],
+            out_send.at[k, 1],
+            line_recv.at[src, j],
             outer_device,
         )
 
     def rest_copy(src, j):
         ref = line.at[src, pl.ds(rows, rows), cols(j)]
-        return remote(ref, ref, rest_send.at[j], line_recv.at[src, j], outer_device)
-
-    def rest_landed(j):
-        landed(line.at[partner_plane, pl.ds(rows, rows), cols(j)], line_recv.at[partner_plane, j])
+        return remote(ref, ref, rest_sem.at[0], rest_sem.at[1], outer_device)
 
     def plane_copy(k, src, j, index):
         ref = tokens.at[device(src, y, c), :, cols(j)]
-        return remote(
-            ref, ref, out_send.at[k, 2 + index, j], token_recv.at[device(src, y, c), j], (beside, twin)[index]
-        )
+        recv = beside_recv.at[src, j] if index == 0 else twin_recv.at[device(src, y, c)]
+        return remote(ref, ref, out_send.at[k, 2 + index], recv, (beside, twin)[index])
 
     def twin_copy(k, src, j):
         there = device(src, 1 - y, c)
         ref = tokens.at[there, :, cols(j)]
-        return remote(ref, ref, out_send.at[k, 4, j], token_recv.at[there, j], twin)
+        return remote(ref, ref, out_send.at[k, 4], twin_recv.at[there], twin)
 
     far = jnp.where(at_end, p + 3 * toward, p + 2 * toward)
     second_plane = jnp.where(at_end, p + 2 * toward, outer)
@@ -525,7 +521,7 @@
             there = device(src, y, c)
             if k > 0:
                 pl.when(at_end)(
-                    lambda: landed(tokens.at[there, :, cols(jj)], token_recv.at[there, jj])
+                    lambda: landed(tokens.at[there, :, cols(jj)], line_recv.at[src, jj])
                 )
                 pl.when(middle)(lambda: landed(line.at[src, :, cols(jj)], line_recv.at[src, jj]))
             if whole is not False:
@@ -555,7 +551,7 @@
 
         def go():
             there = device(src, 1 - y, c)
-            landed(tokens.at[there, :, cols(jj)], token_recv.at[there, jj])
+            landed(tokens.at[there, :, cols(jj)], beside_recv.at[src, jj])
             twin_copy(k, src, jj).start()
 
         pl.when(jnp.logical_and(jj >= 0, jj < chunks))(go)
@@ -600,8 +596,7 @@
         return carry
 
     lax.fori_loop(chunks + BEHIND, chunks + BEHIND + 4 * HOP, drain, 0)
-    for target in others:
-        landed(stats.at[target], stat_recv.at[target])
+    landed(stats.at[pl.ds(0, n - 1)], table_recv.at[1])
     for load in loads[3:]:
         load.wait()
 
@@ -611,15 +606,11 @@
         jnp.where(at_end, inner, outer),
         p,
     ]
-    def arrive(j, carry):
-        for plane in range(planes):
-            for yy in (0, 1):
-                there = device(plane, yy, 1 - c)
-                landed(tokens.at[there, :, cols(j)], token_recv.at[there, j])
-        pl.when(at_end)(lambda: rest_landed(j))
-        return carry
-
-    lax.fori_loop(0, chunks, arrive, 0)
+    for plane in range(planes):
+        for yy in (0, 1):
+            there = device(plane, yy, 1 - c)
+            landed(tokens.at[there], twin_recv.at[there])
+    pl.when(at_end)(lambda: landed(line.at[partner_plane, pl.ds(rows, rows), :], rest_sem.at[1]))
     group = SPLIT * cap
     chunk = 512
     span_back = D // backs
@@ -664,7 +655,7 @@
         return remote(
             block(part, plane * SPLIT + (1 - c) * 2, 2, j),
             block(r1, plane * 2, 2, j),
-            back_send.at[plane, 0, j],
+            back_send.at[plane, 0],
             s1_recv.at[plane, j],
             twin,
         )
@@ -673,7 +664,7 @@
         return remote(
             block(part, plane * SPLIT + c * 2 + 1 - y, 1, j),
             block(r2, plane, 1, j),
-            back_send.at[plane, 1, j],
+            back_send.at[plane, 1],
             s2_recv.at[plane, j],
             beside,
         )
@@ -682,7 +673,7 @@
         return remote(
             pair.at[plane, pl.ds(0, cap), back_cols(j)],
             pair.at[plane, pl.ds(cap, cap), back_cols(j)],
-            back_send.at[plane, 2, j],
+            back_send.at[plane, 2],
             pair_recv.at[plane, j],
             inner_device,
         )
@@ -691,7 +682,7 @@
         return remote(
             acc_out.at[plane, :, back_cols(j)],
             acc_in.at[plane, :, back_cols(j)],
-            back_send.at[plane, 3, j],
+            back_send.at[plane, 3],
             acc_recv.at[plane, j],
             device(jnp.where(plane == outer, outer, inner), y, c),
         )
@@ -773,38 +764,32 @@
 
     lax.fori_loop(0, units + BACK_LAGS[2], give_back, 0)
 
-    def left(j, carry):
-        for i in range(3):
-            over_vertical(i, j).wait_send()
-        pl.when(middle)(rest_copy(inner, j).wait_send)
-        for i in (0, 1):
-            for level in (0, 1):
-                for index, (_, exists) in enumerate(sides):
-                    when(exists, over_side(level, index, i, j).wait_send)
-        for k, (src, _, whole, out) in enumerate(sources):
-            if whole is not False:
-                when(whole, raw_copy(k, src, j).wait_send)
-            if out is not False:
-                when(out, outer_copy(k, src, j).wait_send)
-            for index in (0, 1):
-                plane_copy(k, src, j, index).wait_send()
-            twin_copy(k, src, j).wait_send()
-        return carry
-
-    lax.fori_loop(0, chunks, left, 0)
-    for copy in [tell_column(step) for step in range(planes - 1)] + tell_all():
-        copy.wait_send()
-
-    def returned(j, carry):
-        for plane in range(planes):
-            to_twin(plane, j).wait_send()
-            to_beside(plane, j).wait_send()
-            away = p != plane
-            pl.when(jnp.logical_and(at_end, away))(slots_home(plane, j).wait_send)
-            pl.when(jnp.logical_and(middle, away))(rows_home(plane, j).wait_send)
-        return carry
-
-    lax.fori_loop(0, backs, returned, 0)
+    def gone(ref, sem):
+        remote(ref, ref, sem, own_sem.at[0], twin).wait_send()
+
+    every = pl.ds(0, half)
+    gone(bytes_of(3, every), kv_send.at[0])
+    for level in (0, 1):
+        for index, (_, exists) in enumerate(sides):
+            when(exists, functools.partial(gone, bytes_of(2, every), kv_send.at[1 + level * 2 + index]))
+    for k, (_, _, whole, out) in enumerate(sources):
+        if whole is not False:
+            when(whole, functools.partial(gone, line.at[0], out_send.at[k, 0]))
+        if out is not False:
+            when(out, functools.partial(gone, stage.at[0], out_send.at[k, 1]))
+        for index in range(3):
+            gone(tokens.at[0], out_send.at[k, 2 + index])
+    pl.when(middle)(lambda: gone(line.at[0, pl.ds(0, rows), :], rest_sem.at[0]))
+    gone(tables.at[pl.ds(0, planes - 1)], table_send.at[0])
+    gone(stats.at[pl.ds(0, n - 1)], table_send.at[1])
+    for plane in range(planes):
+        gone(r1.at[pl.ds(0, 2 * cap), :], back_send.at[plane, 0])
+        gone(r1.at[pl.ds(0, cap), :], back_send.at[plane, 1])
+        away = p != plane
+        pl.when(jnp.logical_and(at_end, away))(
+            functools.partial(gone, r1.at[pl.ds(0, cap), :], back_send.at[plane, 2])
+        )
+        pl.when(jnp.logical_and(middle, away))(functools.partial(gone, acc_in.at[0], back_send.at[plane, 3]))
 
 
 def kernel_bytes(n, rows, cap, width):
@@ -854,17 +839,16 @@
             pltpu.VMEM((planes, rows, D), bf),
             pltpu.VMEM((planes, rows, D), bf),
             dma((5,)),
-            dma((11, chunks)),
-            dma((13, chunks)),
-            dma((planes - 1,)),
-            dma((planes,)),
-            dma((n - 1,)),
+            dma((5,)),
+            dma((6, chunks)),
+            dma((2,)),
+            dma((2,)),
+            dma((planes, 5)),
+            dma((planes, chunks)),
+            dma((planes, chunks)),
             dma((n,)),
-            dma((planes, 5, chunks)),
-            dma((planes, chunks)),
-            dma((n, chunks)),
-            dma((chunks,)),
-            dma((planes, 4, backs)),
+            dma((2,)),
+            dma((planes, 4)),
             dma((planes, backs)),
             dma((planes, backs)),
             dma((planes, backs)),

time: 128 us -> 124 us (0.969)
  Pallas kernels: 127 us -> 123 us
    pallas_call x1, Pallas kernels: 127 us -> 123 us  [layer(): pl.pallas_call(functools.partial(layer_kernel, n, rows, cap, CHUNKS, BACK...]
where the time goes in v5:
time: 124 us
  Pallas kernels  123 us (99%)
    pallas_call x1, Pallas kernels, layer(): pl.pallas_call(functools.partial(layer_kernel, n, rows, cap, CHUNKS, BACK...  123 us

profile of v5, /device:TPU:0, one launch (start us, length us, event | category | flops | bytes accessed | tf_op | source)
XLA Modules:
  0.0 123.9 jit_solution(3153957866480416799)
XLA Ops:
  0.0 123.1 %whole_layer.1 = bf16[64,4096]{1,0:T(8,128)(2,1)S(1)} custom-call(bf16[64,4096]{1,0:T(8,128)(2,1)} %q_ref.1, bf16[64,4096]{1,0:T(8,128)(2,1)} %k_ref.1, bf16[64,4096]{1,0:T(8,128)(2,1)} %v_ref.1, f32[3,4096]{1,0:T(4,128)} %mod_ref.1, s32[2,64]{1,0:T(2,128)} %bitcast.2, s32[2,64]{1,0:T(2,128)} %bitcast.3, bf16[4096,512]{1,0:T(8,128)(2,1)} %first_ref.1, ...), custom_call_target="tpu_custom_call" | custom-call | tf_op jit(solution)/shard_map/whole_layer/pallas_call | solution.py:812
  123.1 0.8 copy.10

commit v6 on v5

--- a/solution.py
+++ b/solution.py
@@ -22,6 +22,8 @@
 ASIDE = 2
 BEHIND = 2
 HOP = 2
+DRAIN = (2, 7)
+EARLY = 2
 BACK_CHUNKS = 4
 BACK_LAGS = (1, 4, 6)
 
@@ -378,6 +380,12 @@
             for index, (_, exists) in enumerate(sides):
                 when(exists, over_side(1, index, i, j).start)
 
+    pl.semaphore_wait(barrier, n - 1)
+    send_own(0)
+    send_side(0)
+    for load in loads[:3]:
+        load.start()
+
     expert = lax.broadcasted_iota(jnp.int32, (8, rows), 0)
     named = [routes_ref[k : k + 1, :] == expert for k in (0, 1)]
     member = jnp.logical_or(named[0], named[1])
@@ -394,6 +402,20 @@
     stats[me, 8:16, :] = jnp.where(member, count - 1.0, -1.0)
     tables[me, 8:16, :] = gate / 1024.0
 
+    column_planes = [lax.rem(p + step, planes) for step in range(1, planes)]
+
+    def tell_column(step):
+        there = device(column_planes[step], y, c)
+        return remote(tables.at[me], tables.at[me], table_send.at[0], table_recv.at[0], there)
+
+    for step in range(planes - 1):
+        tell_column(step).start()
+    for j in range(1, max(AHEAD, ASIDE)):
+        if j < min(AHEAD, chunks):
+            send_own(j)
+        if j < min(ASIDE, chunks):
+            send_side(j)
+
     span = 6 * rows
     where = lax.broadcasted_iota(jnp.int32, (8, span), 1)
     penalty = jnp.zeros((8, span), jnp.float32)
@@ -411,30 +433,12 @@
             pl.when(jnp.logical_not(exists))(clear)
     bias[...] = penalty
 
-    column_planes = [lax.rem(p + step, planes) for step in range(1, planes)]
-
-    def tell_column(step):
-        there = device(column_planes[step], y, c)
-        return remote(tables.at[me], tables.at[me], table_send.at[0], table_recv.at[0], there)
-
     def tell_all():
         return [
             remote(stats.at[me], stats.at[me], table_send.at[1], table_recv.at[1], target)
             for target in others
         ]
 
-    pl.semaphore_wait(barrier, n - 1)
-    send_own(0)
-    for step in range(planes - 1):
-        tell_column(step).start()
-    send_side(0)
-    for load in loads[:3]:
-        load.start()
-    for j in range(1, max(AHEAD, ASIDE)):
-        if j < min(AHEAD, chunks):
-            send_own(j)
-        if j < min(ASIDE, chunks):
-            send_side(j)
     for load in loads[:3]:
         load.wait()
     for load in loads[3:]:
@@ -573,6 +577,12 @@
         return carry
 
     lax.fori_loop(0, chunks + BEHIND, stream, 0)
+
+    def drain(j, carry):
+        move(j)
+        return carry
+
+    lax.fori_loop(chunks + BEHIND, chunks + BEHIND + DRAIN[0], drain, 0)
 
     token = lax.broadcasted_iota(jnp.int32, (16, rows), 1)
     line_of = lax.broadcasted_iota(jnp.int32, (16, rows), 0)
@@ -591,26 +601,23 @@
     for copy in tell_all():
         copy.start()
 
-    def drain(j, carry):
-        move(j)
-        return carry
-
-    lax.fori_loop(chunks + BEHIND, chunks + BEHIND + 4 * HOP, drain, 0)
+    lax.fori_loop(chunks + BEHIND + DRAIN[0], chunks + BEHIND + DRAIN[1], drain, 0)
     landed(stats.at[pl.ds(0, n - 1)], table_recv.at[1])
     for load in loads[3:]:
         load.wait()
 
     order = [
+        jnp.where(at_end, p + 2 * toward, inner),
         jnp.where(at_end, p + 3 * toward, p + 2 * toward),
-        jnp.where(at_end, p + 2 * toward, inner),
         jnp.where(at_end, inner, outer),
         p,
     ]
-    for plane in range(planes):
-        for yy in (0, 1):
-            there = device(plane, yy, 1 - c)
-            landed(tokens.at[there], twin_recv.at[there])
-    pl.when(at_end)(lambda: landed(line.at[partner_plane, pl.ds(rows, rows), :], rest_sem.at[1]))
+    def arrive(plane):
+        for source in (plane, lax.rem(plane + planes // 2, planes)):
+            for yy in (0, 1):
+                there = device(source, yy, 1 - c)
+                landed(tokens.at[there], twin_recv.at[there])
+
     group = SPLIT * cap
     chunk = 512
     span_back = D // backs
@@ -689,6 +696,7 @@
 
     def produce(i, j):
         plane = home_of(i)
+        pl.when(jnp.logical_and(j == 0, i < 2))(lambda: arrive(plane))
         pl.when(j == 0)(lambda: start_group(plane))
         raw = jnp.dot(hidden[...], second[:, back_cols(j)], preferred_element_type=jnp.float32)
         mine = pl.ds(pl.multiple_of(plane * group, 16), group)
@@ -751,8 +759,6 @@
         pl.when(jnp.logical_and(middle, i == 2))(lambda: fold(False, True, False))
         pl.when(jnp.logical_and(middle, i < 2))(lambda: fold(True, False, False))
 
-    out_ref[:, halves(mine_from)] = att[:rows, :]
-    out_ref[:, halves(other_from)] = line[partner_plane, rows:, :]
     units = planes * backs
 
     def give_back(u, carry):
@@ -762,7 +768,12 @@
             pl.when(jnp.logical_and(at >= 0, at < units))(functools.partial(act, i, j))
         return carry
 
-    lax.fori_loop(0, units + BACK_LAGS[2], give_back, 0)
+    lax.fori_loop(0, EARLY, give_back, 0)
+    lax.fori_loop(chunks + BEHIND + DRAIN[1], chunks + BEHIND + 4 * HOP, drain, 0)
+    pl.when(at_end)(lambda: landed(line.at[partner_plane, pl.ds(rows, rows), :], rest_sem.at[1]))
+    out_ref[:, halves(mine_from)] = att[:rows, :]
+    out_ref[:, halves(other_from)] = line[partner_plane, rows:, :]
+    lax.fori_loop(EARLY, units + BACK_LAGS[2], give_back, 0)
 
     def gone(ref, sem):
         remote(ref, ref, sem, own_sem.at[0], twin).wait_send()

time: 124 us -> 122 us (0.984)
  Pallas kernels: 123 us -> 121 us
    pallas_call x1, Pallas kernels: 123 us -> 121 us  [layer(): pl.pallas_call(functools.partial(layer_kernel, n, rows, cap, CHUNKS, BACK...]
where the time goes in v6:
time: 122 us
  Pallas kernels  121 us (99%)
    pallas_call x1, Pallas kernels, layer(): pl.pallas_call(functools.partial(layer_kernel, n, rows, cap, CHUNKS, BACK...  121 us

profile of v6, /device:TPU:0, one launch (start us, length us, event | category | flops | bytes accessed | tf_op | source)
XLA Modules:
  0.0 121.6 jit_solution(11344364617762783156)
XLA Ops:
  0.0 120.8 %whole_layer.1 = bf16[64,4096]{1,0:T(8,128)(2,1)S(1)} custom-call(bf16[64,4096]{1,0:T(8,128)(2,1)} %q_ref.1, bf16[64,4096]{1,0:T(8,128)(2,1)} %k_ref.1, bf16[64,4096]{1,0:T(8,128)(2,1)} %v_ref.1, f32[3,4096]{1,0:T(4,128)} %mod_ref.1, s32[2,64]{1,0:T(2,128)} %bitcast.2, s32[2,64]{1,0:T(2,128)} %bitcast.3, bf16[4096,512]{1,0:T(8,128)(2,1)} %first_ref.1, ...), custom_call_target="tpu_custom_call" | custom-call | tf_op jit(solution)/shard_map/whole_layer/pallas_call | solution.py:823
  120.8 0.8 copy.10

commit v7 on v6

--- a/solution.py
+++ b/solution.py
@@ -20,9 +20,10 @@
 CHUNKS = 8
 AHEAD = 2
 ASIDE = 2
-BEHIND = 2
+BEHIND = 1
 HOP = 2
-DRAIN = (2, 7)
+PASS = 4
+DRAIN = (2, 8)
 EARLY = 2
 BACK_CHUNKS = 4
 BACK_LAGS = (1, 4, 6)
@@ -551,7 +552,7 @@
 
     def pass_on(k, j):
         src, behind, _, _ = sources[k]
-        jj = j - behind - HOP
+        jj = j - behind - PASS
 
         def go():
             there = device(src, 1 - y, c)
@@ -769,7 +770,7 @@
         return carry
 
     lax.fori_loop(0, EARLY, give_back, 0)
-    lax.fori_loop(chunks + BEHIND + DRAIN[1], chunks + BEHIND + 4 * HOP, drain, 0)
+    lax.fori_loop(chunks + BEHIND + DRAIN[1], chunks + BEHIND + 3 * HOP + PASS, drain, 0)
     pl.when(at_end)(lambda: landed(line.at[partner_plane, pl.ds(rows, rows), :], rest_sem.at[1]))
     out_ref[:, halves(mine_from)] = att[:rows, :]
     out_ref[:, halves(other_from)] = line[partner_plane, rows:, :]

time: 122 us -> 121 us (level)
  no operation moved by 1% of the time
where the time goes in v7:
time: 121 us
  Pallas kernels  120 us (99%)
    pallas_call x1, Pallas kernels, layer(): pl.pallas_call(functools.partial(layer_kernel, n, rows, cap, CHUNKS, BACK...  120 us

profile of v7, /device:TPU:0, one launch (start us, length us, event | category | flops | bytes accessed | tf_op | source)
XLA Modules:
  0.0 121.0 jit_solution(6839749492730179741)
XLA Ops:
  0.0 120.2 %whole_layer.1 = bf16[64,4096]{1,0:T(8,128)(2,1)S(1)} custom-call(bf16[64,4096]{1,0:T(8,128)(2,1)} %q_ref.1, bf16[64,4096]{1,0:T(8,128)(2,1)} %k_ref.1, bf16[64,4096]{1,0:T(8,128)(2,1)} %v_ref.1, f32[3,4096]{1,0:T(4,128)} %mod_ref.1, s32[2,64]{1,0:T(2,128)} %bitcast.2, s32[2,64]{1,0:T(2,128)} %bitcast.3, bf16[4096,512]{1,0:T(8,128)(2,1)} %first_ref.1, ...), custom_call_target="tpu_custom_call" | custom-call | tf_op jit(solution)/shard_map/whole_layer/pallas_call | solution.py:824
  120.2 0.8 copy.10

commit v8 on v7

--- a/solution.py
+++ b/solution.py
@@ -26,7 +26,7 @@
 DRAIN = (2, 8)
 EARLY = 2
 BACK_CHUNKS = 4
-BACK_LAGS = (1, 4, 6)
+BACK_LAGS = (1, 4, 7)
 
 
 def when(cond, body):
@@ -433,6 +433,7 @@
 
             pl.when(jnp.logical_not(exists))(clear)
     bias[...] = penalty
+    chooser[...] = jnp.zeros(chooser.shape, chooser.dtype)
 
     def tell_all():
         return [
@@ -455,7 +456,6 @@
 
     def choose():
         landed(tables.at[pl.ds(0, planes - 1)], table_recv.at[0])
-        chooser[...] = jnp.zeros(chooser.shape, chooser.dtype)
         for plane in range(planes):
             for place_in, e in ((0, p), (1, outer_expert)):
                 found = chosen(device(plane, y, c), e).astype(jnp.float32).astype(jnp.bfloat16)
@@ -762,7 +762,13 @@
 
     units = planes * backs
 
+    def begin_result():
+        pl.when(at_end)(lambda: landed(line.at[partner_plane, pl.ds(rows, rows), :], rest_sem.at[1]))
+        out_ref[:, halves(mine_from)] = att[:rows, :]
+        out_ref[:, halves(other_from)] = line[partner_plane, rows:, :]
+
     def give_back(u, carry):
+        pl.when(u == 2 * backs + 2)(begin_result)
         for behind, act in ((0, produce), (BACK_LAGS[0], fold_twin), (BACK_LAGS[1], fold_beside), (BACK_LAGS[2], fold_home)):
             at = u - behind
             i, j = lax.div(at, backs), lax.rem(at, backs)
@@ -771,9 +777,6 @@
 
     lax.fori_loop(0, EARLY, give_back, 0)
     lax.fori_loop(chunks + BEHIND + DRAIN[1], chunks + BEHIND + 3 * HOP + PASS, drain, 0)
-    pl.when(at_end)(lambda: landed(line.at[partner_plane, pl.ds(rows, rows), :], rest_sem.at[1]))
-    out_ref[:, halves(mine_from)] = att[:rows, :]
-    out_ref[:, halves(other_from)] = line[partner_plane, rows:, :]
     lax.fori_loop(EARLY, units + BACK_LAGS[2], give_back, 0)
 
     def gone(ref, sem):

time: 121 us -> 121 us (level)
  no operation moved by 1% of the time
where the time goes in v8:
time: 121 us; the launch traced here: 120 us
  Pallas kernels  120 us (99%)
    pallas_call x1, Pallas kernels, layer(): pl.pallas_call(functools.partial(layer_kernel, n, rows, cap, CHUNKS, BACK...  120 us

profile of v8, /device:TPU:0, one launch (start us, length us, event | category | flops | bytes accessed | tf_op | source)
XLA Modules:
  0.0 120.5 jit_solution(9936323683650404134)
XLA Ops:
  0.0 119.7 %whole_layer.1 = bf16[64,4096]{1,0:T(8,128)(2,1)S(1)} custom-call(bf16[64,4096]{1,0:T(8,128)(2,1)} %q_ref.1, bf16[64,4096]{1,0:T(8,128)(2,1)} %k_ref.1, bf16[64,4096]{1,0:T(8,128)(2,1)} %v_ref.1, f32[3,4096]{1,0:T(4,128)} %mod_ref.1, s32[2,64]{1,0:T(2,128)} %bitcast.2, s32[2,64]{1,0:T(2,128)} %bitcast.3, bf16[4096,512]{1,0:T(8,128)(2,1)} %first_ref.1, ...), custom_call_target="tpu_custom_call" | custom-call | tf_op jit(solution)/shard_map/whole_layer/pallas_call | solution.py:827
  119.7 0.8 copy.10

commit v9 on v8

--- a/solution.py
+++ b/solution.py
@@ -23,7 +23,7 @@
 BEHIND = 1
 HOP = 2
 PASS = 4
-DRAIN = (2, 8)
+DRAIN = (1, 8)
 EARLY = 2
 BACK_CHUNKS = 4
 BACK_LAGS = (1, 4, 7)

time: 121 us -> 121 us (level)
  no operation moved by 1% of the time
where the time goes in v9:
time: 121 us; the launch traced here: 120 us
  Pallas kernels  120 us (99%)
    pallas_call x1, Pallas kernels, layer(): pl.pallas_call(functools.partial(layer_kernel, n, rows, cap, CHUNKS, BACK...  120 us

profile of v9, /device:TPU:0, one launch (start us, length us, event | category | flops | bytes accessed | tf_op | source)
XLA Modules:
  0.0 120.5 jit_solution(2922135917227549120)
XLA Ops:
  0.0 119.7 %whole_layer.1 = bf16[64,4096]{1,0:T(8,128)(2,1)S(1)} custom-call(bf16[64,4096]{1,0:T(8,128)(2,1)} %q_ref.1, bf16[64,4096]{1,0:T(8,128)(2,1)} %k_ref.1, bf16[64,4096]{1,0:T(8,128)(2,1)} %v_ref.1, f32[3,4096]{1,0:T(4,128)} %mod_ref.1, s32[2,64]{1,0:T(2,128)} %bitcast.2, s32[2,64]{1,0:T(2,128)} %bitcast.3, bf16[4096,512]{1,0:T(8,128)(2,1)} %first_ref.1, ...), custom_call_target="tpu_custom_call" | custom-call | tf_op jit(solution)/shard_map/whole_layer/pallas_call | solution.py:827
  119.7 0.8 copy.10

commit v10 on v9

--- a/solution.py
+++ b/solution.py
@@ -24,7 +24,7 @@
 HOP = 2
 PASS = 4
 DRAIN = (1, 8)
-EARLY = 2
+EARLY = 3
 BACK_CHUNKS = 4
 BACK_LAGS = (1, 4, 7)
 

time: 121 us -> 121 us (level)
  no operation moved by 1% of the time
where the time goes in v10:
time: 121 us; the launch traced here: 120 us
  Pallas kernels  120 us (99%)
    pallas_call x1, Pallas kernels, layer(): pl.pallas_call(functools.partial(layer_kernel, n, rows, cap, CHUNKS, BACK...  120 us

profile of v10, /device:TPU:0, one launch (start us, length us, event | category | flops | bytes accessed | tf_op | source)
XLA Modules:
  0.0 120.5 jit_solution(14447693411148367016)
XLA Ops:
  0.0 119.7 %whole_layer.1 = bf16[64,4096]{1,0:T(8,128)(2,1)S(1)} custom-call(bf16[64,4096]{1,0:T(8,128)(2,1)} %q_ref.1, bf16[64,4096]{1,0:T(8,128)(2,1)} %k_ref.1, bf16[64,4096]{1,0:T(8,128)(2,1)} %v_ref.1, f32[3,4096]{1,0:T(4,128)} %mod_ref.1, s32[2,64]{1,0:T(2,128)} %bitcast.2, s32[2,64]{1,0:T(2,128)} %bitcast.3, bf16[4096,512]{1,0:T(8,128)(2,1)} %first_ref.1, ...), custom_call_target="tpu_custom_call" | custom-call | tf_op jit(solution)/shard_map/whole_layer/pallas_call | solution.py:827
  119.7 0.8 copy.10
